TPU v7x, 256 devices: a whole 4x4x8 slice. The times are simulated.
256 devices in a mesh: prow: 16 (over z_hi, y, core), pcol: 16 (over x, z_lo).
Axes of the slice: x: 4, y: 4, z: 8 (z_hi: 2, z_lo: 4; z = z_hi * 4 + z_lo), core: 2. Of those that a mesh axis runs over, the one named last changes fastest.
Arguments:
- coords: float32 [2, 8, 8192], P(None, None, 'prow'), may hold values from 0 to 1
- observations: float32 [8, 8192], P(None, 'prow'), may hold values from -6 to 6
- length_scale: float32 [1], replicated, may hold values from 0.06 to 0.15
- nugget: float32 [1], replicated, may hold values from 0.3 to 1
Outputs:
- slab: float32 [8, 8192, 2048], P(None, 'prow', 'pcol')
- whitened: float32 [8, 8192], P(None, 'prow')
- loglik_part: float32 [1], replicated
All inputs are finite; a program needn't handle non-finite values.
Results may differ from a plain program's by a relative error of at most 0.0003.
Values sent between devices are 32-bit elements; how exact they have to be, the bound alone decides.
A program may use at most 128 MiB of HBM per device.

v0:
```python
import math

import jax
import jax.numpy as jnp
from jax import lax
from jax.sharding import PartitionSpec as P

SLAB_DEV = 128


SQRT_THREE = math.sqrt(3.0)


def matern_block(left_xy, right_xy, decay_rate):
    delta_x = left_xy[0][:, None] - right_xy[0][None, :]
    delta_y = left_xy[1][:, None] - right_xy[1][None, :]
    scaled = decay_rate * jnp.sqrt(delta_x * delta_x + delta_y * delta_y)
    return (1.0 + scaled) * jnp.exp(-scaled)


def covariance(left_xy, left_ids, right_xy, right_ids, decay_rate, nugget_value):
    same = (left_ids[:, None] == right_ids[None, :]).astype(jnp.float32)
    return matern_block(left_xy, right_xy, decay_rate) + nugget_value * same


def transposed_product(left, right):
    return jnp.dot(
        left, right.T, precision=lax.Precision.HIGHEST, preferred_element_type=jnp.float32
    )


def vector_product(matrix, vector):
    return jnp.dot(
        matrix, vector, precision=lax.Precision.HIGHEST, preferred_element_type=jnp.float32
    )


def inverse_lower(factor):
    identity = jnp.eye(factor.shape[0], dtype=jnp.float32)
    return jax.scipy.linalg.solve_triangular(factor, identity, lower=True)


def shards(coords, observations, length_scale, nugget):
    row_procs = lax.axis_size("prow")
    col_procs = lax.axis_size("pcol")
    row_rank = lax.axis_index("prow")
    col_rank = lax.axis_index("pcol")
    tile_count = coords.shape[1]
    block_size = coords.shape[2]
    slab_width = SLAB_DEV
    decay_rate = SQRT_THREE / length_scale[0]
    nugget_value = nugget[0]
    leading_xy, leading_obs = (
        lax.all_gather(coords[:, 0, :], "prow", axis=1, tiled=True),
        lax.all_gather(observations[0, :], "prow", axis=0, tiled=True),
    )
    leading_ids = jnp.arange(row_procs * block_size, dtype=jnp.int32)
    first_xy = leading_xy[:, :block_size]
    first_ids = leading_ids[:block_size]
    second_xy = leading_xy[:, block_size : 2 * block_size]
    second_ids = leading_ids[block_size : 2 * block_size]
    factor_first = jnp.linalg.cholesky(
        covariance(first_xy, first_ids, first_xy, first_ids, decay_rate, nugget_value)
    )
    inverse_first = inverse_lower(factor_first)
    second_on_first = transposed_product(
        covariance(second_xy, second_ids, first_xy, first_ids, decay_rate, nugget_value),
        inverse_first,
    )
    schur_second = covariance(
        second_xy, second_ids, second_xy, second_ids, decay_rate, nugget_value
    ) - transposed_product(second_on_first, second_on_first)
    factor_second = jnp.linalg.cholesky(schur_second)
    inverse_second = inverse_lower(factor_second)
    whitened_first = vector_product(inverse_first, leading_obs[:block_size])
    whitened_second = vector_product(
        inverse_second,
        leading_obs[block_size : 2 * block_size] - vector_product(second_on_first, whitened_first),
    )
    quadratic = 0.5 * (
        jnp.sum(whitened_first * whitened_first) + jnp.sum(whitened_second * whitened_second)
    )
    log_terms = jnp.sum(jnp.log(jnp.diagonal(factor_first))) + jnp.sum(
        jnp.log(jnp.diagonal(factor_second))
    )
    loglik_part = -(quadratic + log_terms) / (2.0 * block_size)

    def compute_first(rows_xy, rows_ids):
        raw_rows = transposed_product(
            covariance(rows_xy, rows_ids, first_xy, first_ids, decay_rate, nugget_value),
            inverse_first,
        )
        inside = jnp.take(factor_first, rows_ids % block_size, axis=0)
        return jnp.where((rows_ids < block_size)[:, None], inside, raw_rows)

    def compute_second(rows_xy, rows_ids, rows_first):
        schur_rows = covariance(
            rows_xy, rows_ids, second_xy, second_ids, decay_rate, nugget_value
        ) - transposed_product(rows_first, second_on_first)
        raw_rows = transposed_product(schur_rows, inverse_second)
        inside = jnp.take(factor_second, rows_ids % block_size, axis=0)
        result = jnp.where((rows_ids < 2 * block_size)[:, None], inside, raw_rows)
        return jnp.where((rows_ids < block_size)[:, None], 0.0, result)

    local_xy = coords.reshape(2, tile_count * block_size)
    local_obs = observations.reshape(tile_count * block_size)
    tile_number = jnp.arange(tile_count, dtype=jnp.int32)[:, None]
    offsets = jnp.arange(block_size, dtype=jnp.int32)[None, :]
    local_ids = ((tile_number * row_procs + row_rank) * block_size + offsets).reshape(
        tile_count * block_size
    )
    share_rows = tile_count * block_size // col_procs
    share_first_row = col_rank * share_rows
    share_xy = lax.dynamic_slice_in_dim(local_xy, share_first_row, share_rows, 1)
    share_ids = lax.dynamic_slice_in_dim(local_ids, share_first_row, share_rows, 0)
    share_obs = lax.dynamic_slice_in_dim(local_obs, share_first_row, share_rows, 0)
    column_first_site = 2 * block_size + col_rank * slab_width
    column_xy = lax.dynamic_slice_in_dim(leading_xy, column_first_site, slab_width, 1)
    column_ids = column_first_site + jnp.arange(slab_width, dtype=jnp.int32)
    column_first = compute_first(column_xy, column_ids)
    column_second = compute_second(column_xy, column_ids, column_first)
    share_first = compute_first(share_xy, share_ids)
    local_first = lax.all_gather(share_first, "pcol", axis=0, tiled=True)
    share_second = compute_second(share_xy, share_ids, share_first)
    remainder = (
        share_obs
        - vector_product(share_first, whitened_first)
        - vector_product(share_second, whitened_second)
    )
    inside_first = jnp.take(whitened_first, share_ids % block_size)
    inside_second = jnp.take(whitened_second, share_ids % block_size)
    share_white = jnp.where(
        share_ids < block_size,
        inside_first,
        jnp.where(share_ids < 2 * block_size, inside_second, remainder),
    )
    local_second, local_white = (
        lax.all_gather(share_second, "pcol", axis=0, tiled=True),
        lax.all_gather(share_white, "pcol", axis=0, tiled=True),
    )
    value = covariance(local_xy, local_ids, column_xy, column_ids, decay_rate, nugget_value)
    value = (
        value
        - transposed_product(local_first, column_first)
        - transposed_product(local_second, column_second)
    )
    local_slab = jnp.where((local_ids < 2 * block_size)[:, None], 0.0, value)
    return (
        local_slab.reshape(tile_count, block_size, slab_width),
        local_white.reshape(tile_count, block_size),
        loglik_part.reshape(1),
    )


def solution(mesh):
    placed = (P(None, None, "prow"), P(None, "prow"), P(), P())
    return jax.shard_map(
        shards,
        mesh=mesh,
        in_specs=placed,
        out_specs=(P(None, "prow", "pcol"), P(None, "prow"), P()),
        check_vma=False,
    )
```

profile of v0, /device:TPU:1, one launch (start us, length us, event | category | flops | bytes accessed | tf_op | source)
XLA Modules:
  0.0 581.1 jit_solution(2892677378938574391)
XLA Ops:
  12.0 34.9 %all-gather = f32[2,1,8192]{2,1,0:T(1,128)S(1)} all-gather(f32[2,1,512]{2,1,0:T(1,128)S(1)} %slice.171), channel_id=2, replica_groups=mesh['prow'=16,'pcol'=16] {'prow'}, dimensions={2}, use_global_device_ids=true | all-gather | bytes 69632 | tf_op jit(solution)/shard_map/all_gather | solution.py:54
  49.4 11.7 %cholesky.286 = f32[128,128]{1,0:T(8,128)S(1)} custom-call(f32[128,128]{1,0:T(8,128)S(1)} %cholesky.426), custom_call_target="Cholesky" | custom-call | tf_op jit(solution)/shard_map/jit(cholesky)/cholesky | solution.py:62
  61.2 9.8 %custom-call.31 = f32[1,128,128]{1,2,0:T(8,128)S(1)} custom-call(f32[1,128,128]{2,1,0:T(8,128)S(1)} %get-tuple-element.77), custom_call_target="InvertDiagBlocksLowerTriangular" | custom-call | tf_op jit(solution)/shard_map/jit(cholesky)/cholesky | solution.py:62
  71.8 11.8 %cholesky.305 = f32[128,128]{1,0:T(8,128)S(1)} custom-call(f32[128,128]{1,0:T(8,128)S(1)} %cholesky.430), custom_call_target="Cholesky" | custom-call | tf_op jit(solution)/shard_map/jit(cholesky)/cholesky | solution.py:62
  84.2 9.8 %custom-call.32 = f32[1,128,128]{1,2,0:T(8,128)S(1)} custom-call(f32[1,128,128]{2,1,0:T(8,128)S(1)} %get-tuple-element.74), custom_call_target="InvertDiagBlocksLowerTriangular" | custom-call | tf_op jit(solution)/shard_map/jit(cholesky)/cholesky | solution.py:62
  94.7 11.7 %cholesky.326 = f32[128,128]{1,0:T(8,128)S(1)} custom-call(f32[128,128]{1,0:T(8,128)S(1)} %cholesky.435), custom_call_target="Cholesky" | custom-call | tf_op jit(solution)/shard_map/jit(cholesky)/cholesky | solution.py:62
  107.1 9.8 %custom-call.33 = f32[1,128,128]{1,2,0:T(8,128)S(1)} custom-call(f32[1,128,128]{2,1,0:T(8,128)S(1)} %get-tuple-element.71), custom_call_target="InvertDiagBlocksLowerTriangular" | custom-call | tf_op jit(solution)/shard_map/jit(cholesky)/cholesky | solution.py:62
  117.5 11.9 %cholesky.343 = f32[128,128]{1,0:T(8,128)S(1)} custom-call(f32[128,128]{1,0:T(8,128)S(1)} %convolution_subtract_fusion.16), custom_call_target="Cholesky" | custom-call | tf_op jit(solution)/shard_map/jit(cholesky)/cholesky | solution.py:62
  135.3 11.5 %while.4 = (s32[]{:T(128)}, f32[512,512]{1,0:T(8,128)}, s32[4,2]{0,1:T(2,128)S(1)}, f32[4,128,128]{2,1,0:T(8,128)S(1)}, s32[]{:T(128)}) while((s32[]{:T(128)}, f32[512,512]{1,0:T(8,128)}, s32[4,2]{0,1:T(2,128)S(1)}, f32[4,128,128]{2,1,0:T(8,128)S(1)}, s32[]{:T(128)}) %tuple.70), condition=%wide.while_cond, body=%wide.while_body.sunk | while | flops 2 | bytes 131189 | solution.py:40
  135.9 2.3 bitcast_dynamic-update-slice_fusion.4
  138.8 2.3 bitcast_dynamic-update-slice_fusion.4
  141.7 2.3 bitcast_dynamic-update-slice_fusion.4
  144.6 2.2 bitcast_dynamic-update-slice_fusion.4
  146.8 39.3 %custom-call.34 = f32[4,128,128]{1,2,0:T(8,128)S(1)} custom-call(f32[4,128,128]{2,1,0:T(8,128)S(1)} %get-tuple-element.22), custom_call_target="InvertDiagBlocksLowerTriangular" | custom-call | tf_op jit(solution)/shard_map/jit(_solve_triangular)/triangular_solve | solution.py:40
  190.1 1.7 convolution_subtract_fusion.9
  194.0 3.1 convolution_select_fusion.1
  197.7 5.0 fusion.7
  203.7 2.4 convolution_subtract_fusion.2
  210.1 11.7 %cholesky.358 = f32[128,128]{1,0:T(8,128)S(1)} custom-call(f32[128,128]{1,0:T(8,128)S(1)} %cholesky.439), custom_call_target="Cholesky" | custom-call | tf_op jit(solution)/shard_map/jit(cholesky)/cholesky | solution.py:73
  222.3 10.0 %custom-call.35 = f32[1,128,128]{1,2,0:T(8,128)S(1)} custom-call(f32[1,128,128]{2,1,0:T(8,128)S(1)} %get-tuple-element.61), custom_call_target="InvertDiagBlocksLowerTriangular" | custom-call | tf_op jit(solution)/shard_map/jit(cholesky)/cholesky | solution.py:73
  235.6 11.7 %cholesky.377 = f32[128,128]{1,0:T(8,128)S(1)} custom-call(f32[128,128]{1,0:T(8,128)S(1)} %cholesky.443), custom_call_target="Cholesky" | custom-call | tf_op jit(solution)/shard_map/jit(cholesky)/cholesky | solution.py:73
  247.9 9.8 %custom-call.36 = f32[1,128,128]{1,2,0:T(8,128)S(1)} custom-call(f32[1,128,128]{2,1,0:T(8,128)S(1)} %get-tuple-element.58), custom_call_target="InvertDiagBlocksLowerTriangular" | custom-call | tf_op jit(solution)/shard_map/jit(cholesky)/cholesky | solution.py:73
  260.9 13.2 %cholesky.398 = f32[128,128]{1,0:T(8,128)} custom-call(f32[128,128]{1,0:T(8,128)} %cholesky.448), custom_call_target="Cholesky" | custom-call | tf_op jit(solution)/shard_map/jit(cholesky)/cholesky | solution.py:73
  274.0 2.0 select_reduce_fusion.1
  276.0 11.5 %custom-call.37 = f32[1,128,128]{1,2,0:T(8,128)} custom-call(f32[1,128,128]{2,1,0:T(8,128)} %get-tuple-element.55), custom_call_target="InvertDiagBlocksLowerTriangular" | custom-call | tf_op jit(solution)/shard_map/jit(cholesky)/cholesky | solution.py:73
  289.8 12.4 %cholesky.415 = f32[128,128]{1,0:T(8,128)} custom-call(f32[128,128]{1,0:T(8,128)S(1)} %convolution_subtract_fusion.15), custom_call_target="Cholesky" | custom-call | tf_op jit(solution)/shard_map/jit(cholesky)/cholesky | solution.py:73
  310.3 2.6 fusion.5
  313.6 14.5 %while.5 = (s32[]{:T(128)}, f32[512,512]{1,0:T(8,128)}, s32[4,2]{0,1:T(2,128)S(1)}, f32[4,128,128]{2,1,0:T(8,128)}, s32[]{:T(128)}) while((s32[]{:T(128)}, f32[512,512]{1,0:T(8,128)}, s32[4,2]{0,1:T(2,128)S(1)}, f32[4,128,128]{2,1,0:T(8,128)}, s32[]{:T(128)}) %tuple.80), condition=%wide.while_cond.clone, body=%wide.while_body.clone.sunk | while | flops 2 | bytes 132205 | solution.py:40
  314.6 2.9 bitcast_dynamic-update-slice_fusion.5
  318.2 2.9 bitcast_dynamic-update-slice_fusion.5
  321.7 2.9 bitcast_dynamic-update-slice_fusion.5
  325.2 2.8 bitcast_dynamic-update-slice_fusion.5
  328.1 40.8 %custom-call.38 = f32[4,128,128]{1,2,0:T(8,128)} custom-call(f32[4,128,128]{2,1,0:T(8,128)} %get-tuple-element.23), custom_call_target="InvertDiagBlocksLowerTriangular" | custom-call | tf_op jit(solution)/shard_map/jit(_solve_triangular)/triangular_solve | solution.py:40
  368.8 1.8 gather_fusion.4
  376.6 1.7 convolution_subtract_fusion.8
  380.1 1.9 fusion.1
  382.1 6.7 %gather_fusion = f32[512]{0:T(512)} fusion(f32[512,512]{1,0:T(8,128)S(1)} %get-tuple-element.45, s32[512]{0:T(512)S(1)} %bitcast.177), kind=kCustom, calls=%fused_computation.6 | custom fusion | bytes 8192 | tf_op jit(solution)/shard_map/jit(diagonal)/cond/branch_0_fun/gather | solution.py:83
  388.8 6.8 %gather_fusion.1 = f32[512]{0:T(512)} fusion(f32[512,512]{1,0:T(8,128)S(1)} %get-tuple-element.41, s32[512]{0:T(512)S(1)} %bitcast.178), kind=kCustom, calls=%fused_computation.7 | custom fusion | bytes 8192 | tf_op jit(solution)/shard_map/jit(diagonal)/cond/branch_0_fun/gather | solution.py:84
  398.6 25.0 %all-gather.1 = f32[1,8192]{1,0:T(1,128)S(1)} all-gather(f32[1,512]{1,0:T(1,128)S(1)} %slice.183), channel_id=3, replica_groups=mesh['prow'=16,'pcol'=16] {'prow'}, dimensions={1}, use_global_device_ids=true | all-gather | bytes 34816 | tf_op jit(solution)/shard_map/all_gather | solution.py:55
  423.6 2.0 fusion.136
  425.6 2.1 gather_fusion.6
  428.9 2.0 fusion.101
  430.9 2.0 gather_fusion.7
  439.1 36.9 %all-gather.2 = f32[16,1,256]{2,1,0:T(1,128)S(1)} all-gather(f32[1,1,256]{2,1,0:T(1,128)S(1)} %bitcast.212), channel_id=1, replica_groups=mesh['prow'=16,'pcol'=16] {'pcol'}, dimensions={0}, use_global_device_ids=true | all-gather | bytes 17408 | tf_op jit(solution)/shard_map/all_gather | solution.py:139
  477.3 2.5 convolution_select_fusion.3
  482.3 9.5 %convolution_subtract_fusion.1 = f32[4096,128]{1,0:T(8,128)S(1)} fusion(f32[4096,512]{1,0:T(8,128)} %all-gather.6.cloned.1.call-done, f32[128,512]{1,0:T(8,128)S(1)} %convolution_select_fusion.3, f32[]{:T(128)} %bitcast.164, s32[128]{0:T(128)S(1)} %iota_add_fusion.2, f32[128]{0:T(128)S(1)} %get-tuple-element.67, f32[4096]{0:T(1024)S(1)} %bitcast.184, ...), kind=kOutput, calls=%fused_computation.14 | convolution fusion | flops 3228041216 | bytes 10798600 | tf_op jit(solution)/shard_map/dot_general | solution.py:27
  491.9 71.0 %all-gather.8.cloned.1.call-done = f32[4096,512]{1,0:T(8,128)} async-done(((f32[256,512]{1,0:T(8,128)}), f32[4096,512]{1,0:T(8,128)}) %all-gather.8.cloned.1.call-update) | async-done | bytes 8388624 | tf_op jit(solution)/shard_map/all_gather | solution.py:138
  562.9 10.1 %fusion = f32[4096,128]{1,0:T(8,128)} fusion(f32[4096,128]{1,0:T(8,128)S(1)} %convolution_subtract_fusion.1, f32[4096,512]{1,0:T(8,128)} %all-gather.8.cloned.1.call-done, f32[128,512]{1,0:T(8,128)S(1)} %fusion.2, pred[4096]{0:T(1024)(128)(4,1)S(1)} %broadcast_compare_fusion), kind=kOutput, calls=%fused_computation.13 | convolution fusion | flops 3222274048 | bytes 12849152 | tf_op jit(solution)/shard_map/dot_general | solution.py:27
  (240 shorter events, 64.1 us)
Async XLA Ops:
  7.2 475.2 %all-gather.6.cloned.1.call-start = ((), (), s32[]{:S(2)}) async-start(), calls=%async_computation | async-start | bytes 8912896 | tf_op jit(solution)/shard_map/all_gather | solution.py:123
  7.8 189.9 %copy-start.27 = (s32[512]{0:T(512)}, s32[512]{0:T(512)S(1)}, u32[]{:S(2)}) copy-start(s32[512]{0:T(512)S(1)} %iota_add_fusion.1) | copy-start | bytes 6148
  10.6 183.3 %copy-start.44 = (s32[256]{0:T(256)}, s32[256]{0:T(256)S(1)}, u32[]{:S(2)}) copy-start(s32[256]{0:T(256)S(1)} %get-tuple-element.43) | copy-start | bytes 3076
  11.2 181.8 %copy-start.34 = (s32[1024]{0:T(1024)}, s32[1024]{0:T(1024)S(1)}, u32[]{:S(2)}) copy-start(s32[1024]{0:T(1024)S(1)} %pad_clamp_fusion.1) | copy-start | bytes 12292
  46.9 150.7 %copy-start.29 = (f32[1,512]{1,0:T(1,128)}, f32[1,512]{1,0:T(1,128)S(1)}, u32[]{:S(2)}) copy-start(f32[1,512]{1,0:T(1,128)S(1)} %get-tuple-element.63) | copy-start | bytes 6148
  47.0 150.7 %copy-start.31 = (f32[1,512]{1,0:T(1,128)}, f32[1,512]{1,0:T(1,128)S(1)}, u32[]{:S(2)}) copy-start(f32[1,512]{1,0:T(1,128)S(1)} %get-tuple-element.64) | copy-start | bytes 6148
  47.0 155.8 %copy-start.38 = (f32[1,512]{1,0:T(1,128)}, f32[1,512]{1,0:T(1,128)S(1)}, u32[]{:S(2)}) copy-start(f32[1,512]{1,0:T(1,128)S(1)} %get-tuple-element.62) | copy-start | bytes 6148
  47.0 155.8 %copy-start.40 = (f32[1,512]{1,0:T(1,128)}, f32[1,512]{1,0:T(1,128)S(1)}, u32[]{:S(2)}) copy-start(f32[1,512]{1,0:T(1,128)S(1)} %get-tuple-element.65) | copy-start | bytes 6148
  94.7 40.6 %copy-start.58 = (s32[4]{0:T(128)S(1)}, s32[4]{0:T(128)}, u32[]{:S(2)}) copy-start(s32[4]{0:T(128)} %iota_multiply_fusion) | copy-start | bytes 52
  146.8 44.9 %copy-start.25 = (s32[4,2]{0,1:T(2,128)}, s32[4,2]{0,1:T(2,128)S(1)}, u32[]{:S(2)}) copy-start(s32[4,2]{0,1:T(2,128)S(1)} %get-tuple-element.189) | copy-start | bytes 100
  188.2 9.5 %copy-start.7 = (f32[128,512]{1,0:T(8,128)}, f32[128,512]{1,0:T(8,128)S(1)}, u32[]{:S(2)}) copy-start(f32[128,512]{1,0:T(8,128)S(1)} %fusion.127) | copy-start | bytes 786436
  190.1 7.6 %copy-start.14 = (f32[128,512]{1,0:T(8,128)}, f32[128,512]{1,0:T(8,128)S(1)}, u32[]{:S(2)}) copy-start(f32[128,512]{1,0:T(8,128)S(1)} %fusion.125) | copy-start | bytes 786436
  197.2 365.7 %all-gather.8.cloned.1.call-start = ((), (), s32[]{:S(2)}) async-start(), calls=%async_computation.1 | async-start | bytes 8912896 | tf_op jit(solution)/shard_map/all_gather | solution.py:138
  197.6 5.1 copy-start.36
  288.6 25.0 %copy-start.26 = (s32[4,2]{0,1:T(2,128)S(1)}, s32[4,2]{0,1:T(2,128)}, u32[]{:S(2)}) copy-start(s32[4,2]{0,1:T(2,128)} %copy-done.25) | copy-start | bytes 100
  310.3 58.5 %copy-start.35 = (s32[1024]{0:T(1024)S(1)}, s32[1024]{0:T(1024)}, u32[]{:S(2)}) copy-start(s32[1024]{0:T(1024)} %copy-done.34) | copy-start | bytes 12292
  370.6 5.5 copy-start.21
  371.9 8.2 %copy-start.4 = (f32[128,512]{1,0:T(8,128)}, f32[128,512]{1,0:T(8,128)S(1)}, u32[]{:S(2)}) copy-start(f32[128,512]{1,0:T(8,128)S(1)} %fusion.89) | copy-start | bytes 786436
  373.2 5.5 copy-start.2
  373.2 5.5 copy-start.11
  373.2 5.5 copy-start.37
  373.2 5.5 copy-start.39
  373.2 5.5 copy-start.41
  373.3 5.5 copy-start.45
  373.3 5.5 copy-start.55
  373.3 5.5 copy-start.57
  374.7 5.4 copy-start.9
  376.5 3.6 copy-start.15
  376.6 3.6 copy-start.18
  376.6 3.6 copy-start.46
  395.6 28.0 %copy-start.24 = (f32[2,8,512]{2,1,0:T(8,128)S(1)}, f32[2,8,512]{2,1,0:T(8,128)}, u32[]{:S(2)}) copy-start(f32[2,8,512]{2,1,0:T(8,128)} %param.13) | copy-start | bytes 98308
  397.1 26.5 %copy-start.8 = (f32[128,512]{1,0:T(8,128)S(1)}, f32[128,512]{1,0:T(8,128)}, u32[]{:S(2)}) copy-start(f32[128,512]{1,0:T(8,128)} %copy-done.7) | copy-start | bytes 786436
  398.5 29.2 %copy-start.3 = (f32[512,512]{1,0:T(8,128)S(1)}, f32[512,512]{1,0:T(8,128)}, u32[]{:S(2)}) copy-start(f32[512,512]{1,0:T(8,128)} %copy-done.1) | copy-start | bytes 3145732
  398.5 30.3 %copy-start.5 = (f32[128,512]{1,0:T(8,128)S(1)}, f32[128,512]{1,0:T(8,128)}, u32[]{:S(2)}) copy-start(f32[128,512]{1,0:T(8,128)} %copy-done.4) | copy-start | bytes 786436
  398.5 30.3 %copy-start.10 = (f32[128,512]{1,0:T(8,128)S(1)}, f32[128,512]{1,0:T(8,128)}, u32[]{:S(2)}) copy-start(f32[128,512]{1,0:T(8,128)} %copy-done.9) | copy-start | bytes 786436
  427.8 5.1 copy-start.43
  427.8 5.7 copy-start.42
  427.8 10.1 %copy-start.12 = (f32[256,512]{1,0:T(8,128)S(1)}, f32[256,512]{1,0:T(8,128)}, u32[]{:S(2)}) copy-start(f32[256,512]{1,0:T(8,128)} %convolution_select_fusion.1) | copy-start | bytes 1572868
  427.8 10.6 %copy-start.13 = (f32[256,512]{1,0:T(8,128)S(1)}, f32[256,512]{1,0:T(8,128)}, u32[]{:S(2)}) copy-start(f32[256,512]{1,0:T(8,128)} %fusion.1) | copy-start | bytes 1572868
  428.8 10.1 %copy-start.47 = (pred[256]{0:T(512)(128)(4,1)S(1)}, pred[256]{0:T(512)(128)(4,1)}, u32[]{:S(2)}) copy-start(pred[256]{0:T(512)(128)(4,1)} %get-tuple-element.42) | copy-start | bytes 772
  428.8 10.2 %copy-start.50 = (pred[256]{0:T(512)(128)(4,1)S(1)}, pred[256]{0:T(512)(128)(4,1)}, u32[]{:S(2)}) copy-start(pred[256]{0:T(512)(128)(4,1)} %get-tuple-element.46) | copy-start | bytes 772
  428.8 10.2 %copy-start.53 = (pred[256]{0:T(512)(128)(4,1)S(1)}, pred[256]{0:T(512)(128)(4,1)}, u32[]{:S(2)}) copy-start(pred[256]{0:T(512)(128)(4,1)} %get-tuple-element.82) | copy-start | bytes 772
  428.8 48.4 %copy-start.28 = (s32[512]{0:T(512)S(1)}, s32[512]{0:T(512)}, u32[]{:S(2)}) copy-start(s32[512]{0:T(512)} %copy-done.27) | copy-start | bytes 6148
  428.8 48.4 %copy-start.30 = (f32[1,512]{1,0:T(1,128)S(1)}, f32[1,512]{1,0:T(1,128)}, u32[]{:S(2)}) copy-start(f32[1,512]{1,0:T(1,128)} %copy-done.29) | copy-start | bytes 6148
  428.8 48.4 %copy-start.32 = (f32[1,512]{1,0:T(1,128)S(1)}, f32[1,512]{1,0:T(1,128)}, u32[]{:S(2)}) copy-start(f32[1,512]{1,0:T(1,128)} %copy-done.31) | copy-start | bytes 6148
  477.3 3.8 copy-start.16
  477.3 3.8 copy-start.20
  477.3 3.8 copy-start.23
  (13 other events, 22.2 us)
Sparse Core Ops, SparseCore 0:
  197.3 179.6 all-gather.5
  382.2 180.6 all-gather.7
where the time goes:
time: 592 us; the launch traced here: 581 us
  other arithmetic  260 us (44%)
  blocking collectives  96.7 us (16%)
  waiting for transfers between devices  71 us (12%)
  matrix products  68 us (11%)
  local copies, waits for them, and re-layouts  58.5 us (10%)
  between operations  25.7 us (4%)
    another operation x15, other arithmetic, shards(): factor_second = jnp.linalg.cholesky(schur_second)  88.9 us
    another operation x5, other arithmetic, inverse_lower(): return jax.scipy.linalg.solve_triangular(factor, identity, lower=True)  84.4 us
    another operation x14, other arithmetic, shards(): jnp.linalg.cholesky(covariance(first_xy, first_ids, first_xy, first_ids,...  79.9 us
    all_gather x1, waiting for transfers between devices, shards(): lax.all_gather(share_second, 'pcol', axis=0, tiled=True)  71 us
    dot_general x10, matrix products, transposed_product(): jnp.dot(left, right.T, precision=lax.Precision.HIGHEST, preferred_element...  38.3 us
    all_gather x1, blocking collectives, shards(): lax.all_gather(share_white, 'pcol', axis=0, tiled=True)  36.9 us
    all_gather x1, blocking collectives, shards(): lax.all_gather(coords[:, 0, :], 'prow', axis=1, tiled=True)  34.9 us
    another operation x27, local copies, waits for them, and re-layouts, inverse_lower(): return jax.scipy.linalg.solve_triangular(factor, identity, lower=True)  26.3 us
  transfers between devices with their start and end apart: 2, of which 1 were waited for; matrix products, arithmetic and copies ran while one was open for 38% of the time, Pallas kernels for 0%

commit v1 on v0

v1 whole, which is shorter than its diff:
```python
import math

import jax
import jax.numpy as jnp
from jax import lax
from jax.experimental import pallas as pl
from jax.experimental.pallas import tpu as pltpu
from jax.sharding import PartitionSpec as P

SQRT_THREE = math.sqrt(3.0)
F32 = jnp.float32
BF16 = jnp.bfloat16
MESH = pl.DeviceIdType.MESH

B = 512
T = 2 * B
NB = 128
NK = T // NB
N_PROW = 16
TILES = 8
NC = 128
WIDTH = T + 2 * NC


def gather_kernel(pk_ref, t_ref, c_ref, t0, t1, tc, send_sem, recv_sem):
    prow = lax.axis_index("prow")
    pcol = lax.axis_index("pcol")
    col_owner = 2 + pcol // 4
    part = pl.ds(pl.multiple_of((pcol % 4) * NC, NC), NC)
    barrier = pltpu.get_barrier_semaphore()
    senders = ((0, 0), (1, 1), (col_owner, 2))
    for owner, _ in senders:
        @pl.when(prow != owner)
        def _():
            pl.semaphore_signal(barrier, inc=1, device_id=(owner, pcol), device_id_type=MESH)

    sources = (pk_ref, pk_ref, pk_ref.at[:, part])
    slots = (t0, t1, tc)

    def copy(slot, step, target):
        return pltpu.make_async_remote_copy(
            src_ref=sources[slot], dst_ref=slots[slot],
            send_sem=send_sem.at[step], recv_sem=recv_sem.at[slot],
            device_id=(target, pcol), device_id_type=MESH)

    for owner, slot in senders:
        @pl.when(prow == owner)
        def _():
            pl.semaphore_wait(barrier, N_PROW - 1)
            for step in range(1, N_PROW):
                copy(slot, step, (prow + step) % N_PROW).start()
            slots[slot][...] = sources[slot][...]
            for step in range(1, N_PROW):
                copy(slot, step, (prow + step) % N_PROW).wait_send()
    for owner, slot in senders:
        @pl.when(prow != owner)
        def _():
            copy(slot, 1, (prow + 1) % N_PROW).wait_recv()
    t_ref[:, :B] = t0[...]
    t_ref[:, B:] = t1[...]
    c_ref[...] = tc[...]


def gather_sites(pk):
    vm = pl.BlockSpec(memory_space=pltpu.VMEM)
    return pl.pallas_call(
        gather_kernel,
        out_shape=(jax.ShapeDtypeStruct((4, T), F32), jax.ShapeDtypeStruct((4, NC), F32)),
        in_specs=[vm], out_specs=(vm, vm),
        scratch_shapes=[
            pltpu.VMEM((4, B), F32), pltpu.VMEM((4, B), F32), pltpu.VMEM((4, NC), F32),
            pltpu.SemaphoreType.DMA((N_PROW,)), pltpu.SemaphoreType.DMA((3,)),
        ],
        compiler_params=pltpu.CompilerParams(collective_id=0, has_side_effects=True),
        name="gather_sites",
    )(pk)


def split(x):
    high = x.astype(BF16)
    return high, (x - high.astype(F32)).astype(BF16)


def matern(dx, dy):
    q = jnp.maximum(dx * dx + dy * dy, 1e-30)
    s = q * lax.rsqrt(q)
    return (1.0 + s) * jnp.exp(-s)


def lanes(x, j):
    return jnp.broadcast_to(x[:, j:j + 1], (8, 128))


def rows(x, i):
    return jnp.broadcast_to(x[i:i + 1, :], (8, 128))


def mm(x, y):
    return lax.dot_general(x, y, (((1,), (0,)), ((), ())), preferred_element_type=F32)


def mm3(x, y):
    xh, xl = split(x)
    yh, yl = split(y)
    return mm(jnp.concatenate([xh, xh, xl], 1), jnp.concatenate([yh, yl, yh], 0))


def factor_block(load, store):
    lane = lax.broadcasted_iota(jnp.int32, (8, 128), 1)
    sub = lax.broadcasted_iota(jnp.int32, (8, 128), 0)
    a = [load(i) for i in range(16)]
    pivots = jnp.ones((8, 128), F32)
    for b in range(16):
        w_out = jnp.zeros((8, 128), F32)
        for h in range(2):
            j0 = 8 * b + 4 * h
            pivot_lanes = (lane >= j0) & (lane < j0 + 4)
            eye = (lane - j0) == (sub - 4 * h)
            r = a[b]
            cb = [lanes(r, j0 + t) for t in range(4)]
            s = {(i, t): rows(cb[t], 4 * h + i) for t in range(4) for i in range(t, 4)}
            rpp = jnp.where(pivot_lanes, jnp.where(eye, 1.0, 0.0), r)
            rb = [rows(rpp, 4 * h + t) for t in range(4)]
            rp = []
            l = {}
            for t in range(4):
                rp.append(1.0 / s[t, t])
                for i in range(t + 1, 4):
                    l[i, t] = s[i, t] * rp[t]
                for i in range(t + 1, 4):
                    for c in range(t + 1, i + 1):
                        s[i, c] = s[i, c] - l[i, t] * s[c, t]
                    rb[i] = rb[i] - l[i, t] * rb[t]
            for t in range(4):
                pivots = jnp.where(lane == j0 + t, s[t, t], pivots)
                w = jnp.where(lane < j0 + 4, rb[t] * lax.rsqrt(s[t, t]), 0.0)
                w_out = jnp.where(sub == 4 * h + t, w, w_out)
            x = [None] * 4
            for t in (3, 2, 1, 0):
                x[t] = rb[t] * rp[t]
                for i in range(t + 1, 4):
                    x[t] = x[t] - l[i, t] * x[i]
            for i in range(b if h == 0 else b + 1, 16):
                c = cb if i == b else [lanes(a[i], j0 + t) for t in range(4)]
                new = jnp.where(pivot_lanes, 0.0, a[i]) - (
                    (c[0] * x[0] + c[1] * x[1]) + (c[2] * x[2] + c[3] * x[3]))
                a[i] = jnp.where(sub >= 4, new, a[i]) if i == b else new
        store(b, w_out)
    return pivots


def main_kernel(ls_ref, ng_ref, co_ref, ob_ref, t_ref, c_ref,
                slab_ref, white_ref, ll_ref,
                a_ref, w_ref, wt_ref, yh_ref, yl_ref, yb_ref, z_ref, m_ref,
                rx_ref, ry_ref, mc_ref, wv_ref, ld_ref, flat_ref):
    prow = lax.axis_index("prow")
    pcol = lax.axis_index("pcol")
    rate = SQRT_THREE / jnp.full((1, 128), ls_ref[0], F32)
    nugget = ng_ref[0]
    lane = lax.broadcasted_iota(jnp.int32, (8, 128), 1)
    sub = lax.broadcasted_iota(jnp.int32, (8, 128), 0)
    rate_t = jnp.concatenate([rate] * 8, 1)
    tx = t_ref[0:1, :] * rate_t
    ty = t_ref[1:2, :] * rate_t
    cx = c_ref[0:1, :] * rate
    cy = c_ref[1:2, :] * rate
    ux = [tx[:, 128 * i:128 * i + 128] for i in range(8)] + [cx]
    uy = [ty[:, 128 * i:128 * i + 128] for i in range(8)] + [cy]

    for q in range(TILES):
        for i in range(4):
            part = slice(128 * i, 128 * i + 128)
            at = slice(q * B + 128 * i, q * B + 128 * i + 128)
            rx_ref[at, :] = jnp.broadcast_to(co_ref[0, q:q + 1, part] * rate, (128, 128)).T
            ry_ref[at, :] = jnp.broadcast_to(co_ref[1, q:q + 1, part] * rate, (128, 128)).T
            flat_ref[4 * q + i:4 * q + i + 1, :] = ob_ref[q:q + 1, part]

    for k in range(NK):
        part = slice(128 * k, 128 * k + 128)
        px = jnp.broadcast_to(tx[:, part], (128, 128)).T
        py = jnp.broadcast_to(ty[:, part], (128, 128)).T
        w_ref[0] = px
        w_ref[1] = py
        wide = lax.broadcasted_iota(jnp.int32, (128, 128), 1)
        a_ref[k, :, T + NC:] = jnp.where(
            wide == 0, jnp.broadcast_to(t_ref[2:3, part], (128, 128)).T, 0.0)

        def build(g, carry, k=k):
            at = pl.ds(pl.multiple_of(8 * g, 8), 8)
            gx = w_ref[0, at, :]
            gy = w_ref[1, at, :]
            for j in range(k, 9):
                v = matern(gx - ux[j], gy - uy[j])
                if j == k:
                    v = v + jnp.where(lane == sub + 8 * g, nugget, 0.0)
                a_ref[k, at, 128 * j:128 * j + 128] = v
            return carry
        lax.fori_loop(0, 16, build, 0)

    ld_ref[...] = jnp.zeros((8, 128), F32)

    def step(k, carry):
        off = pl.ds(pl.multiple_of(128 * k, 128), 128)

        def load(i):
            return a_ref[k, 8 * i:8 * i + 8, off]

        def store(i, w):
            w_ref[k, 8 * i:8 * i + 8, :] = w

        pivots = factor_block(load, store)
        ld_ref[...] = ld_ref[...] + jnp.log(pivots)
        for kk in range(NK):
            @pl.when(k == kk)
            def _():
                o = 128 * (kk + 1)
                n = WIDTH - o
                w = w_ref[kk]
                wt_ref[kk] = w.T
                y = mm3(w, a_ref[kk, :, o:])
                yh, yl = split(y)
                if kk < NK - 1:
                    yh_ref[kk, :, o:T] = yh[:, :n - 256]
                    yl_ref[kk, :, o:T] = yl[:, :n - 256]
                yb_ref[kk] = y[:, n - 256:]
                z_ref[kk:kk + 1, :] = y[:, n - 128:].T[0:1, :]
                ycat = jnp.concatenate([yh, yl, yh], 0)
                for i in range(kk + 1, NK):
                    f = 128 * (i - kk - 1)
                    th, tl = split(y[:, f:f + 128].T)
                    tcat = jnp.concatenate([th, th, tl], 1)
                    a_ref[i, :, 128 * i:] = a_ref[i, :, 128 * i:] - mm(tcat, ycat[:, f:])
        return carry
    lax.fori_loop(0, NK, step, 0)

    for k in range(NK - 1, -1, -1):
        acc = yb_ref[k]
        if k < NK - 1:
            o = 128 * (k + 1)
            mh, ml = split(m_ref[o:, :])
            yh = yh_ref[k, :, o:T]
            acc = acc - (mm(yh, mh) + mm(yh, ml) + mm(yl_ref[k, :, o:T], mh))
        m_ref[128 * k:128 * k + 128, :] = mm3(wt_ref[k], acc)

    mh, ml = split(m_ref[:, :NC])
    mc_ref[:, :NC] = mh
    mc_ref[:, NC:] = ml
    wt = m_ref[:, NC:].T
    wh, wl = split(wt[0:1, :])
    wv_ref[...] = jnp.concatenate([wh, wl, jnp.zeros((14, T), BF16)], 0)

    z = z_ref[...]
    total = jnp.sum(z * z) + jnp.sum(ld_ref[0:1, :])
    ll_ref[...] = jnp.full((1, 128), total * (-0.5 / T), F32)

    def body(r, carry):
        q = r // 4
        j = r % 4
        at = pl.ds(pl.multiple_of(128 * r, 128), 128)
        gx = rx_ref[at, :]
        gy = ry_ref[at, :]
        acc = None
        for t in range(4):
            piece = jnp.concatenate(
                [matern(gx - ux[2 * t + e], gy - uy[2 * t + e]) for e in range(2)], 1)
            ch, cl = split(piece)
            mt = mc_ref[256 * t:256 * t + 256, :]
            wv = wv_ref[:, 256 * t:256 * t + 256]
            both = mm(ch, mt)
            low = mm(cl, mt[:, :NC])
            wr = lax.dot_general(wv, ch, (((1,), (1,)), ((), ())), preferred_element_type=F32)
            wr2 = lax.dot_general(wv, cl, (((1,), (1,)), ((), ())), preferred_element_type=F32)
            cur = (both[:, :NC] + both[:, NC:] + low, wr[0:1] + wr[1:2] + wr2[0:1])
            acc = cur if acc is None else (acc[0] + cur[0], acc[1] + cur[1])
        panel = (q == 0) & (prow < 2)
        first = (q * N_PROW + prow) * B + 128 * j - (T + pcol * NC)
        wl_ = lax.broadcasted_iota(jnp.int32, (128, 128), 1)
        ws_ = lax.broadcasted_iota(jnp.int32, (128, 128), 0)
        value = matern(gx - cx, gy - cy) + jnp.where(wl_ == ws_ + first, nugget, 0.0) - acc[0]
        slab_ref[q, pl.ds(pl.multiple_of(128 * j, 128), 128), :] = jnp.where(panel, 0.0, value)
        zr = z_ref[pl.ds(jnp.minimum(prow, 1) * 4 + j, 1), :]
        flat_ref[pl.ds(r, 1), :] = jnp.where(panel, zr, flat_ref[pl.ds(r, 1), :] - acc[1])
        return carry
    lax.fori_loop(0, 32, body, 0)
    for r in range(32):
        white_ref[r // 4:r // 4 + 1, 128 * (r % 4):128 * (r % 4) + 128] = flat_ref[r:r + 1, :]


def main_call(length_scale, nugget, coords, observations, sites, columns):
    vm = pl.BlockSpec(memory_space=pltpu.VMEM)
    sm = pl.BlockSpec(memory_space=pltpu.SMEM)
    return pl.pallas_call(
        main_kernel,
        out_shape=(jax.ShapeDtypeStruct((TILES, B, NC), F32),
                   jax.ShapeDtypeStruct((TILES, B), F32),
                   jax.ShapeDtypeStruct((1, 128), F32)),
        in_specs=[sm, sm, vm, vm, vm, vm], out_specs=(vm, vm, vm),
        scratch_shapes=[
            pltpu.VMEM((NK, NB, WIDTH), F32),
            pltpu.VMEM((NK, NB, NB), F32),
            pltpu.VMEM((NK, NB, NB), F32),
            pltpu.VMEM((NK, NB, T), BF16),
            pltpu.VMEM((NK, NB, T), BF16),
            pltpu.VMEM((NK, NB, 2 * NC), F32),
            pltpu.VMEM((NK, NB), F32),
            pltpu.VMEM((T, 2 * NC), F32),
            pltpu.VMEM((TILES * B, 128), F32),
            pltpu.VMEM((TILES * B, 128), F32),
            pltpu.VMEM((T, 2 * NC), BF16),
            pltpu.VMEM((16, T), BF16),
            pltpu.VMEM((8, 128), F32),
            pltpu.VMEM((32, 128), F32),
        ],
        compiler_params=pltpu.CompilerParams(vmem_limit_bytes=60 * 1024 * 1024),
        name="factor_and_slab",
    )(length_scale, nugget, coords, observations, sites, columns)


def shards(coords, observations, length_scale, nugget):
    pk = jnp.concatenate([coords[:, 0, :], observations[0:1], observations[0:1]], 0)
    sites, columns = gather_sites(pk)
    slab, white, ll = main_call(length_scale, nugget, coords, observations, sites, columns)
    return slab, white, ll[0, :1]


def solution(mesh):
    placed = (P(None, None, "prow"), P(None, "prow"), P(), P())
    return jax.shard_map(
        shards,
        mesh=mesh,
        in_specs=placed,
        out_specs=(P(None, "prow", "pcol"), P(None, "prow"), P()),
        check_vma=False,
    )
```

time: 592 us -> 106 us (0.18); the launches traced: 581 us -> 106 us
  other arithmetic: 260 us -> 0.61 us
  Pallas kernels: 0 us -> 102 us
  blocking collectives: 96.7 us -> 0 us
  waiting for transfers between devices: 71 us -> 0 us
  matrix products: 68 us -> 0 us
  local copies, waits for them, and re-layouts: 58.5 us -> 1.49 us
  between operations: 25.7 us -> 1.93 us
    another operation x34 -> x0, other arithmetic: 253 us -> none  [the longest x15 88.9 us: shards(): factor_second = jnp.linalg.cholesky(schur_second)]
    pallas_call x0 -> x2, Pallas kernels: none -> 102 us  [the longest x1 87.1 us: main_call(): pl.pallas_call(main_kernel, out_shape=(jax.ShapeDtypeStruct((TILES, B, NC...]
    all_gather x3 -> x0, blocking collectives: 96.7 us -> none  [the longest x1 36.9 us: shards(): lax.all_gather(share_white, 'pcol', axis=0, tiled=True)]
    all_gather x2 -> x0, waiting for transfers between devices: 71 us -> none  [the longest x1 71 us: shards(): lax.all_gather(share_second, 'pcol', axis=0, tiled=True)]
    dot_general x15 -> x0, matrix products: 44.3 us -> none  [the longest x10 38.3 us: transposed_product(): jnp.dot(left, right.T, precision=lax.Precision.HIGHEST, preferred_element...]
    another operation x35 -> x0, local copies, waits for them, and re-layouts: 27.2 us -> none  [the longest x27 26.3 us: inverse_lower(): return jax.scipy.linalg.solve_triangular(factor, identity, lower=True)]
    another operation x26 -> x0, matrix products: 23.7 us -> none  [the longest x14 14.6 us: inverse_lower(): return jax.scipy.linalg.solve_triangular(factor, identity, lower=True)]
    gather x8 -> x0, local copies, waits for them, and re-layouts: 23.2 us -> none  [the longest x1 6.77 us: shards(): jnp.diagonal(factor_second)]
  transfers between devices with their start and end apart: 2 -> 0, of which waited for: 1 -> 0; matrix products, arithmetic and copies ran while one was open for 38% -> 0% of each run, Pallas kernels for 0% -> 0%
where the time goes in v1:
time: 106 us
  Pallas kernels  102 us (96%)
  between operations  1.93 us (2%)
  local copies, waits for them, and re-layouts  1.49 us (1%)
    pallas_call x1, Pallas kernels, main_call(): pl.pallas_call(main_kernel, out_shape=(jax.ShapeDtypeStruct((TILES, B, NC...  87.1 us
    pallas_call x1, Pallas kernels, gather_sites(): pl.pallas_call(gather_kernel, out_shape=(jax.ShapeDtypeStruct((4, T), F32...  14.7 us

profile of v1, /device:TPU:1, one launch (start us, length us, event | category | flops | bytes accessed | tf_op | source)
XLA Modules:
  0.0 105.8 jit_solution(10425234906832350142)
XLA Ops:
  1.9 0.7 slice.11
  2.6 0.8 slice.10
  3.4 0.6 pad_maximum_fusion.pk_ref
  4.0 14.7 %gather_sites.1 = (f32[4,1024]{1,0:T(4,128)}, f32[4,128]{1,0:T(4,128)}) custom-call(f32[4,512]{1,0:T(4,128)} %pad_maximum_fusion.pk_ref), custom_call_target="tpu_custom_call" | custom-call | tf_op jit(solution)/shard_map/gather_sites/pallas_call | solution.py:66
  18.7 87.1 %factor_and_slab.1 = (f32[8,512,128]{2,1,0:T(8,128)}, f32[8,512]{1,0:T(8,128)}, f32[1,128]{1,0:T(1,128)}) custom-call(f32[1]{0:T(128)S(6)} %copy.11.ls_ref, f32[1]{0:T(128)S(6)} %copy.12.ng_ref, f32[2,8,512]{2,1,0:T(8,128)} %co_ref.1, f32[8,512]{1,0:T(8,128)} %ob_ref.1, f32[4,1024]{1,0:T(4,128)} %get-tuple-element.8.t_ref, f32[4,128]{1,0:T(4,128)} %get-tuple-element.9.c_ref), custom_call_target="tpu_custom_call" | custom-call | tf_op jit(solution)/shard_map/factor_and_slab/pallas_call | solution.py:292
  (1 shorter events, 0.0 us)

commit v2 on v1

--- a/solution.py
+++ b/solution.py
@@ -8,6 +8,7 @@
 from jax.sharding import PartitionSpec as P
 
 SQRT_THREE = math.sqrt(3.0)
+MINUS_LOG2E = -math.log2(math.e)
 F32 = jnp.float32
 BF16 = jnp.bfloat16
 MESH = pl.DeviceIdType.MESH
@@ -82,9 +83,8 @@
 
 
 def matern(dx, dy):
-    q = jnp.maximum(dx * dx + dy * dy, 1e-30)
-    s = q * lax.rsqrt(q)
-    return (1.0 + s) * jnp.exp(-s)
+    s = 1.0 / lax.rsqrt(dx * dx + dy * dy)
+    return (1.0 + s) * jnp.exp2(s * MINUS_LOG2E)
 
 
 def lanes(x, j):
@@ -92,7 +92,7 @@
 
 
 def rows(x, i):
-    return jnp.broadcast_to(x[i:i + 1, :], (8, 128))
+    return jnp.take_along_axis(x, jnp.full((8, 128), i, jnp.int32), axis=0)
 
 
 def mm(x, y):
@@ -121,6 +121,13 @@
             s = {(i, t): rows(cb[t], 4 * h + i) for t in range(4) for i in range(t, 4)}
             rpp = jnp.where(pivot_lanes, jnp.where(eye, 1.0, 0.0), r)
             rb = [rows(rpp, 4 * h + t) for t in range(4)]
+            nx = b if h == 0 else b + 1
+            if h == 0:
+                cn = [jnp.where(sub >= 4, c, 0.0) for c in cb]
+            elif nx < 16:
+                cn = [lanes(a[nx], j0 + t) for t in range(4)]
+            else:
+                cn = None
             rp = []
             l = {}
             for t in range(4):
@@ -129,8 +136,19 @@
                     l[i, t] = s[i, t] * rp[t]
                 for i in range(t + 1, 4):
                     for c in range(t + 1, i + 1):
-                        s[i, c] = s[i, c] - l[i, t] * s[c, t]
+                        if c == t + 1 and i == c:
+                            s[i, c] = s[i, c] - (s[i, t] * s[i, t]) * rp[t]
+                        else:
+                            s[i, c] = s[i, c] - l[i, t] * s[c, t]
                     rb[i] = rb[i] - l[i, t] * rb[t]
+                    if cn is not None:
+                        cn[i] = cn[i] - l[i, t] * cn[t]
+            if cn is not None:
+                base = jnp.where(pivot_lanes, 0.0, a[nx])
+                if h == 0:
+                    base = jnp.where(sub >= 4, base, a[nx])
+                part = [(cn[t] * rp[t]) * rb[t] for t in range(4)]
+                a[nx] = ((base - part[0]) - (part[1] + part[2])) - part[3]
             for t in range(4):
                 pivots = jnp.where(lane == j0 + t, s[t, t], pivots)
                 w = jnp.where(lane < j0 + 4, rb[t] * lax.rsqrt(s[t, t]), 0.0)
@@ -140,11 +158,10 @@
                 x[t] = rb[t] * rp[t]
                 for i in range(t + 1, 4):
                     x[t] = x[t] - l[i, t] * x[i]
-            for i in range(b if h == 0 else b + 1, 16):
-                c = cb if i == b else [lanes(a[i], j0 + t) for t in range(4)]
-                new = jnp.where(pivot_lanes, 0.0, a[i]) - (
+            for i in range(nx + 1, 16):
+                c = [lanes(a[i], j0 + t) for t in range(4)]
+                a[i] = jnp.where(pivot_lanes, 0.0, a[i]) - (
                     (c[0] * x[0] + c[1] * x[1]) + (c[2] * x[2] + c[3] * x[3]))
-                a[i] = jnp.where(sub >= 4, new, a[i]) if i == b else new
         store(b, w_out)
     return pivots
 
@@ -253,35 +270,35 @@
     total = jnp.sum(z * z) + jnp.sum(ld_ref[0:1, :])
     ll_ref[...] = jnp.full((1, 128), total * (-0.5 / T), F32)
 
-    def body(r, carry):
-        q = r // 4
-        j = r % 4
-        at = pl.ds(pl.multiple_of(128 * r, 128), 128)
-        gx = rx_ref[at, :]
-        gy = ry_ref[at, :]
-        acc = None
-        for t in range(4):
-            piece = jnp.concatenate(
-                [matern(gx - ux[2 * t + e], gy - uy[2 * t + e]) for e in range(2)], 1)
-            ch, cl = split(piece)
-            mt = mc_ref[256 * t:256 * t + 256, :]
-            wv = wv_ref[:, 256 * t:256 * t + 256]
-            both = mm(ch, mt)
-            low = mm(cl, mt[:, :NC])
-            wr = lax.dot_general(wv, ch, (((1,), (1,)), ((), ())), preferred_element_type=F32)
-            wr2 = lax.dot_general(wv, cl, (((1,), (1,)), ((), ())), preferred_element_type=F32)
-            cur = (both[:, :NC] + both[:, NC:] + low, wr[0:1] + wr[1:2] + wr2[0:1])
-            acc = cur if acc is None else (acc[0] + cur[0], acc[1] + cur[1])
+    wl_ = lax.broadcasted_iota(jnp.int32, (128, 128), 1)
+    ws_ = lax.broadcasted_iota(jnp.int32, (128, 128), 0)
+
+    def body(q, carry):
         panel = (q == 0) & (prow < 2)
-        first = (q * N_PROW + prow) * B + 128 * j - (T + pcol * NC)
-        wl_ = lax.broadcasted_iota(jnp.int32, (128, 128), 1)
-        ws_ = lax.broadcasted_iota(jnp.int32, (128, 128), 0)
-        value = matern(gx - cx, gy - cy) + jnp.where(wl_ == ws_ + first, nugget, 0.0) - acc[0]
-        slab_ref[q, pl.ds(pl.multiple_of(128 * j, 128), 128), :] = jnp.where(panel, 0.0, value)
-        zr = z_ref[pl.ds(jnp.minimum(prow, 1) * 4 + j, 1), :]
-        flat_ref[pl.ds(r, 1), :] = jnp.where(panel, zr, flat_ref[pl.ds(r, 1), :] - acc[1])
+        for j in range(4):
+            at = pl.ds(pl.multiple_of(512 * q + 128 * j, 128), 128)
+            gx = rx_ref[at, :]
+            gy = ry_ref[at, :]
+            acc = None
+            for t in range(4):
+                piece = jnp.concatenate(
+                    [matern(gx - ux[2 * t + e], gy - uy[2 * t + e]) for e in range(2)], 1)
+                ch, cl = split(piece)
+                mt = mc_ref[256 * t:256 * t + 256, :]
+                wv = wv_ref[:, 256 * t:256 * t + 256]
+                both = mm(ch, mt)
+                low = mm(cl, mt[:, :NC])
+                wr = lax.dot_general(wv, ch, (((1,), (1,)), ((), ())), preferred_element_type=F32)
+                wr2 = lax.dot_general(wv, cl, (((1,), (1,)), ((), ())), preferred_element_type=F32)
+                cur = (both[:, :NC] + both[:, NC:] + low, wr[0:1] + wr[1:2] + wr2[0:1])
+                acc = cur if acc is None else (acc[0] + cur[0], acc[1] + cur[1])
+            first = (q * N_PROW + prow) * B + 128 * j - (T + pcol * NC)
+            value = matern(gx - cx, gy - cy) + jnp.where(wl_ == ws_ + first, nugget, 0.0) - acc[0]
+            slab_ref[q, 128 * j:128 * j + 128, :] = jnp.where(panel, 0.0, value)
+            zr = z_ref[pl.ds(jnp.minimum(prow, 1) * 4 + j, 1), :]
+            flat_ref[pl.ds(4 * q + j, 1), :] = jnp.where(panel, zr, flat_ref[pl.ds(4 * q + j, 1), :] - acc[1])
         return carry
-    lax.fori_loop(0, 32, body, 0)
+    lax.fori_loop(0, TILES, body, 0)
     for r in range(32):
         white_ref[r // 4:r // 4 + 1, 128 * (r % 4):128 * (r % 4) + 128] = flat_ref[r:r + 1, :]
 

time: 106 us -> 82 us (0.77)
  Pallas kernels: 102 us -> 77.7 us
    pallas_call x1, Pallas kernels: 87.1 us -> 63 us  [main_call(): pl.pallas_call(main_kernel, out_shape=(jax.ShapeDtypeStruct((TILES, B, NC...]
where the time goes in v2:
time: 82 us; the launch traced here: 81.7 us
  Pallas kernels  77.7 us (95%)
  between operations  1.93 us (2%)
  local copies, waits for them, and re-layouts  1.49 us (2%)
    pallas_call x1, Pallas kernels, main_call(): pl.pallas_call(main_kernel, out_shape=(jax.ShapeDtypeStruct((TILES, B, NC...  63 us
    pallas_call x1, Pallas kernels, gather_sites(): pl.pallas_call(gather_kernel, out_shape=(jax.ShapeDtypeStruct((4, T), F32...  14.7 us

profile of v2, /device:TPU:1, one launch (start us, length us, event | category | flops | bytes accessed | tf_op | source)
XLA Modules:
  0.0 81.7 jit_solution(11267233911253919256)
XLA Ops:
  1.9 0.7 slice.11
  2.6 0.8 slice.10
  3.4 0.6 pad_maximum_fusion.pk_ref
  4.0 14.7 %gather_sites.1 = (f32[4,1024]{1,0:T(4,128)}, f32[4,128]{1,0:T(4,128)}) custom-call(f32[4,512]{1,0:T(4,128)} %pad_maximum_fusion.pk_ref), custom_call_target="tpu_custom_call" | custom-call | tf_op jit(solution)/shard_map/gather_sites/pallas_call | solution.py:67
  18.7 63.0 %factor_and_slab.1 = (f32[8,512,128]{2,1,0:T(8,128)}, f32[8,512]{1,0:T(8,128)}, f32[1,128]{1,0:T(1,128)}) custom-call(f32[1]{0:T(128)S(6)} %copy.11.ls_ref, f32[1]{0:T(128)S(6)} %copy.12.ng_ref, f32[2,8,512]{2,1,0:T(8,128)} %co_ref.1, f32[8,512]{1,0:T(8,128)} %ob_ref.1, f32[4,1024]{1,0:T(4,128)} %get-tuple-element.8.t_ref, f32[4,128]{1,0:T(4,128)} %get-tuple-element.9.c_ref), custom_call_target="tpu_custom_call" | custom-call | tf_op jit(solution)/shard_map/factor_and_slab/pallas_call | solution.py:309
  (1 shorter events, 0.0 us)

commit v3 on v2

--- a/solution.py
+++ b/solution.py
@@ -16,6 +16,8 @@
 B = 512
 T = 2 * B
 NB = 128
+SP = 64
+PW = 16
 NK = T // NB
 N_PROW = 16
 TILES = 8
@@ -105,71 +107,64 @@
     return mm(jnp.concatenate([xh, xh, xl], 1), jnp.concatenate([yh, yl, yh], 0))
 
 
-def factor_block(load, store):
+def factor_block(d_ref, w_ref, k):
     lane = lax.broadcasted_iota(jnp.int32, (8, 128), 1)
     sub = lax.broadcasted_iota(jnp.int32, (8, 128), 0)
-    a = [load(i) for i in range(16)]
-    pivots = jnp.ones((8, 128), F32)
-    for b in range(16):
-        w_out = jnp.zeros((8, 128), F32)
-        for h in range(2):
-            j0 = 8 * b + 4 * h
-            pivot_lanes = (lane >= j0) & (lane < j0 + 4)
-            eye = (lane - j0) == (sub - 4 * h)
-            r = a[b]
-            cb = [lanes(r, j0 + t) for t in range(4)]
-            s = {(i, t): rows(cb[t], 4 * h + i) for t in range(4) for i in range(t, 4)}
-            rpp = jnp.where(pivot_lanes, jnp.where(eye, 1.0, 0.0), r)
-            rb = [rows(rpp, 4 * h + t) for t in range(4)]
-            nx = b if h == 0 else b + 1
-            if h == 0:
-                cn = [jnp.where(sub >= 4, c, 0.0) for c in cb]
-            elif nx < 16:
-                cn = [lanes(a[nx], j0 + t) for t in range(4)]
-            else:
-                cn = None
-            rp = []
-            l = {}
-            for t in range(4):
-                rp.append(1.0 / s[t, t])
-                for i in range(t + 1, 4):
-                    l[i, t] = s[i, t] * rp[t]
-                for i in range(t + 1, 4):
-                    for c in range(t + 1, i + 1):
-                        if c == t + 1 and i == c:
-                            s[i, c] = s[i, c] - (s[i, t] * s[i, t]) * rp[t]
+    wide = lax.broadcasted_iota(jnp.int32, (SP, 128), 1)
+    nv = SP // 8
+    logs = jnp.zeros((8, 128), F32)
+    for p in range(NB // SP):
+        r0 = SP * p
+        a = [d_ref[r0 + 8 * i:r0 + 8 * i + 8, :] for i in range(nv)]
+        d = [jnp.ones((8, 128), F32) for _ in range(nv)]
+        for c0 in range(0, SP, PW):
+            own = range(c0 // 8, (c0 + PW) // 8)
+            cols = {(t, v): lanes(a[v], r0 + t)
+                    for t in range(c0, c0 + PW) for v in range(t // 8, nv)}
+            group = (lane >= r0 + c0) & (lane < r0 + c0 + PW)
+            for v in range(c0 // 8, nv):
+                fill = jnp.where((lane - r0) == (sub + 8 * v), 1.0, 0.0) if v in own else 0.0
+                a[v] = jnp.where(group, fill, a[v])
+            for t in range(c0, c0 + PW):
+                vt, st = t // 8, t % 8
+                pivot = rows(cols[t, vt], st)
+                d[vt] = jnp.where(sub == st, pivot, d[vt])
+                rp = 1.0 / pivot
+                m = {v: cols[t, v] * rp for v in range(vt, nv)}
+                for i in range(t + 1, c0 + PW):
+                    entry = rows(cols[t, i // 8], i % 8)
+                    for v in range(i // 8, nv):
+                        if i == t + 1 and v == i // 8:
+                            cols[i, v] = cols[i, v] - (cols[t, v] * entry) * rp
                         else:
-                            s[i, c] = s[i, c] - l[i, t] * s[c, t]
-                    rb[i] = rb[i] - l[i, t] * rb[t]
-                    if cn is not None:
-                        cn[i] = cn[i] - l[i, t] * cn[t]
-            if cn is not None:
-                base = jnp.where(pivot_lanes, 0.0, a[nx])
-                if h == 0:
-                    base = jnp.where(sub >= 4, base, a[nx])
-                part = [(cn[t] * rp[t]) * rb[t] for t in range(4)]
-                a[nx] = ((base - part[0]) - (part[1] + part[2])) - part[3]
-            for t in range(4):
-                pivots = jnp.where(lane == j0 + t, s[t, t], pivots)
-                w = jnp.where(lane < j0 + 4, rb[t] * lax.rsqrt(s[t, t]), 0.0)
-                w_out = jnp.where(sub == 4 * h + t, w, w_out)
-            x = [None] * 4
-            for t in (3, 2, 1, 0):
-                x[t] = rb[t] * rp[t]
-                for i in range(t + 1, 4):
-                    x[t] = x[t] - l[i, t] * x[i]
-            for i in range(nx + 1, 16):
-                c = [lanes(a[i], j0 + t) for t in range(4)]
-                a[i] = jnp.where(pivot_lanes, 0.0, a[i]) - (
-                    (c[0] * x[0] + c[1] * x[1]) + (c[2] * x[2] + c[3] * x[3]))
-        store(b, w_out)
-    return pivots
+                            cols[i, v] = cols[i, v] - m[v] * entry
+                row = rows(a[vt], st)
+                for v in range(vt, nv):
+                    mv = jnp.where(sub > st, m[v], 0.0) if v == vt else m[v]
+                    a[v] = a[v] - mv * row
+        y_out = []
+        for v in range(nv):
+            y = a[v] * lax.rsqrt(d[v])
+            logs = logs + jnp.log(d[v])
+            y_out.append(jnp.where((lane > r0 + 8 * v + sub) & (lane < r0 + SP), 0.0, y))
+        y = jnp.concatenate(y_out, 0)
+        w_ref[k, r0:r0 + SP, :] = jnp.where(wide < r0 + SP, y, 0.0)
+        if r0 + SP < NB:
+            yh, yl = split(y)
+            left = jnp.concatenate([yh.astype(F32), yh.astype(F32), yl.astype(F32)], 0).T
+            left = left[r0 + SP:, :].astype(BF16)
+            update = mm(left, jnp.concatenate([yh, yl, yh], 0))
+            rest = d_ref[r0 + SP:, :]
+            own = lax.broadcasted_iota(jnp.int32, rest.shape, 1)
+            own = (own >= r0) & (own < r0 + SP)
+            d_ref[r0 + SP:, :] = jnp.where(own, 0.0, rest) - update
+    return logs
 
 
 def main_kernel(ls_ref, ng_ref, co_ref, ob_ref, t_ref, c_ref,
                 slab_ref, white_ref, ll_ref,
                 a_ref, w_ref, wt_ref, yh_ref, yl_ref, yb_ref, z_ref, m_ref,
-                rx_ref, ry_ref, mc_ref, wv_ref, ld_ref, flat_ref):
+                rx_ref, ry_ref, mc_ref, wv_ref, ld_ref, flat_ref, d_ref):
     prow = lax.axis_index("prow")
     pcol = lax.axis_index("pcol")
     rate = SQRT_THREE / jnp.full((1, 128), ls_ref[0], F32)
@@ -219,14 +214,8 @@
     def step(k, carry):
         off = pl.ds(pl.multiple_of(128 * k, 128), 128)
 
-        def load(i):
-            return a_ref[k, 8 * i:8 * i + 8, off]
-
-        def store(i, w):
-            w_ref[k, 8 * i:8 * i + 8, :] = w
-
-        pivots = factor_block(load, store)
-        ld_ref[...] = ld_ref[...] + jnp.log(pivots)
+        d_ref[...] = a_ref[k, :, off]
+        ld_ref[...] = ld_ref[...] + factor_block(d_ref, w_ref, k)
         for kk in range(NK):
             @pl.when(k == kk)
             def _():
@@ -267,7 +256,7 @@
     wv_ref[...] = jnp.concatenate([wh, wl, jnp.zeros((14, T), BF16)], 0)
 
     z = z_ref[...]
-    total = jnp.sum(z * z) + jnp.sum(ld_ref[0:1, :])
+    total = jnp.sum(z * z) + jnp.sum(ld_ref[:, 0:1])
     ll_ref[...] = jnp.full((1, 128), total * (-0.5 / T), F32)
 
     wl_ = lax.broadcasted_iota(jnp.int32, (128, 128), 1)
@@ -327,6 +316,7 @@
             pltpu.VMEM((16, T), BF16),
             pltpu.VMEM((8, 128), F32),
             pltpu.VMEM((32, 128), F32),
+            pltpu.VMEM((NB, NB), F32),
         ],
         compiler_params=pltpu.CompilerParams(vmem_limit_bytes=60 * 1024 * 1024),
         name="factor_and_slab",

time: 82 us -> 67.7 us (0.83)
  Pallas kernels: 77.7 us -> 63.4 us
    pallas_call x1, Pallas kernels: 63 us -> 48.7 us  [main_call(): pl.pallas_call(main_kernel, out_shape=(jax.ShapeDtypeStruct((TILES, B, NC...]
where the time goes in v3:
time: 67.7 us; the launch traced here: 67.4 us
  Pallas kernels  63.4 us (94%)
  between operations  1.93 us (3%)
  local copies, waits for them, and re-layouts  1.49 us (2%)
    pallas_call x1, Pallas kernels, main_call(): pl.pallas_call(main_kernel, out_shape=(jax.ShapeDtypeStruct((TILES, B, NC...  48.7 us
    pallas_call x1, Pallas kernels, gather_sites(): pl.pallas_call(gather_kernel, out_shape=(jax.ShapeDtypeStruct((4, T), F32...  14.7 us

profile of v3, /device:TPU:1, one launch (start us, length us, event | category | flops | bytes accessed | tf_op | source)
XLA Modules:
  0.0 67.4 jit_solution(12537342977517518210)
XLA Ops:
  1.9 0.7 %slice.11 = f32[1,512]{1,0:T(1,128)S(1)} slice(f32[8,512]{1,0:T(8,128)} %ob_ref.1), slice={[0:1], [0:512]} | slice | bytes 4096 | tf_op jit(solution)/shard_map/slice | solution.py:327
  2.6 0.8 %slice.10 = f32[2,1,512]{2,1,0:T(1,128)S(1)} slice(f32[2,8,512]{2,1,0:T(8,128)} %co_ref.1), slice={[0:2], [0:1], [0:512]} | slice | bytes 8192 | tf_op jit(solution)/shard_map/slice | solution.py:327
  3.4 0.6 pad_maximum_fusion.pk_ref
  4.0 14.7 %gather_sites.1 = (f32[4,1024]{1,0:T(4,128)}, f32[4,128]{1,0:T(4,128)}) custom-call(f32[4,512]{1,0:T(4,128)} %pad_maximum_fusion.pk_ref), custom_call_target="tpu_custom_call" | custom-call | tf_op jit(solution)/shard_map/gather_sites/pallas_call | solution.py:69
  18.7 48.7 %factor_and_slab.1 = (f32[8,512,128]{2,1,0:T(8,128)}, f32[8,512]{1,0:T(8,128)}, f32[1,128]{1,0:T(1,128)}) custom-call(f32[1]{0:T(128)S(6)} %copy.11.ls_ref, f32[1]{0:T(128)S(6)} %copy.12.ng_ref, f32[2,8,512]{2,1,0:T(8,128)} %co_ref.1, f32[8,512]{1,0:T(8,128)} %ob_ref.1, f32[4,1024]{1,0:T(4,128)} %get-tuple-element.8.t_ref, f32[4,128]{1,0:T(4,128)} %get-tuple-element.9.c_ref), custom_call_target="tpu_custom_call" | custom-call | tf_op jit(solution)/shard_map/factor_and_slab/pallas_call | solution.py:298
  (1 shorter events, 0.0 us)

commit v4 on v3

--- a/solution.py
+++ b/solution.py
@@ -20,63 +20,136 @@
 PW = 16
 NK = T // NB
 N_PROW = 16
+HALF = 8
 TILES = 8
 NC = 128
 WIDTH = T + 2 * NC
 
 
-def gather_kernel(pk_ref, t_ref, c_ref, t0, t1, tc, send_sem, recv_sem):
+def gather_kernel(co_ref, ob_ref, t_ref, c_ref, xy0, xy1, xyc, ob0, ob1,
+                  send_sem, relay_sem, recv_sem, own_sem):
     prow = lax.axis_index("prow")
     pcol = lax.axis_index("pcol")
-    col_owner = 2 + pcol // 4
-    part = pl.ds(pl.multiple_of((pcol % 4) * NC, NC), NC)
+    half = prow // HALF
+    local = prow % HALF
+    line = (pcol // 4) * 4
+    zlo = pcol % 4
+    near = line + jnp.where(zlo < 2, 3, 0)
+    feeds = jnp.where(zlo == 3, 0, 2)
+    feeder = (half == 0) & ((zlo == 0) | (zlo == 3))
+    owners = (0, 1, 2 + pcol // 4)
+
+    def part(z):
+        return pl.ds(pl.multiple_of(z * NC, NC), NC)
+
+    def pieces(slot, z):
+        if slot == 2:
+            return ((co_ref.at[:, 0:1, part(z)], xyc.at[:, 0:1, :]),)
+        xy, ob = ((xy0, ob0), (xy1, ob1))[slot]
+        return ((co_ref.at[:, 0:1, :], xy.at[:, 0:1, :]), (ob_ref.at[0:1, :], ob.at[0:1, :]))
+
     barrier = pltpu.get_barrier_semaphore()
-    senders = ((0, 0), (1, 1), (col_owner, 2))
-    for owner, _ in senders:
-        @pl.when(prow != owner)
+    for slot, owner in enumerate(owners):
+        @pl.when(local != owner)
         def _():
-            pl.semaphore_signal(barrier, inc=1, device_id=(owner, pcol), device_id_type=MESH)
-
-    sources = (pk_ref, pk_ref, pk_ref.at[:, part])
-    slots = (t0, t1, tc)
-
-    def copy(slot, step, target):
+            pl.semaphore_signal(barrier, inc=1, device_id=(half * HALF + owner, pcol),
+                                device_id_type=MESH)
+
+        @pl.when((local == owner) & (half == 1))
+        def _():
+            pl.semaphore_signal(barrier, inc=1, device_id=(owner, near), device_id_type=MESH)
+
+    def remote(slot, piece, src, dst, sem, target):
         return pltpu.make_async_remote_copy(
-            src_ref=sources[slot], dst_ref=slots[slot],
-            send_sem=send_sem.at[step], recv_sem=recv_sem.at[slot],
-            device_id=(target, pcol), device_id_type=MESH)
-
-    for owner, slot in senders:
-        @pl.when(prow == owner)
+            src_ref=src, dst_ref=dst, send_sem=sem, recv_sem=recv_sem.at[slot, piece],
+            device_id=target, device_id_type=MESH)
+
+    def spread(slot, owner, from_slot):
+        out = []
+        for step in range(1, HALF):
+            target = (half * HALF + (local + step) % HALF, pcol)
+            for n, (src, dst) in enumerate(pieces(slot, zlo)):
+                out.append(remote(slot, n, dst if from_slot else src, dst,
+                                  send_sem.at[step, n], target))
+        return out
+
+    def feed(slot):
+        out = []
+        for e in range(2):
+            target = (prow + HALF, line + feeds + e)
+            for n, (src, dst) in enumerate(pieces(slot, feeds + e)):
+                out.append(remote(slot, n, src, dst, relay_sem.at[e, n], target))
+        return out
+
+    for slot, owner in enumerate(owners):
+        @pl.when((local == owner) & (half == 0))
         def _():
-            pl.semaphore_wait(barrier, N_PROW - 1)
-            for step in range(1, N_PROW):
-                copy(slot, step, (prow + step) % N_PROW).start()
-            slots[slot][...] = sources[slot][...]
-            for step in range(1, N_PROW):
-                copy(slot, step, (prow + step) % N_PROW).wait_send()
-    for owner, slot in senders:
-        @pl.when(prow != owner)
+            @pl.when(feeder)
+            def _():
+                pl.semaphore_wait(barrier, HALF + 1)
+                for c in feed(slot):
+                    c.start()
+
+            @pl.when(jnp.logical_not(feeder))
+            def _():
+                pl.semaphore_wait(barrier, HALF - 1)
+            for c in spread(slot, owner, False):
+                c.start()
+            mine = [pltpu.make_async_copy(src, dst, own_sem.at[n])
+                    for n, (src, dst) in enumerate(pieces(slot, zlo))]
+            for c in mine:
+                c.start()
+            for c in mine:
+                c.wait()
+            for c in spread(slot, owner, False):
+                c.wait_send()
+
+            @pl.when(feeder)
+            def _():
+                for c in feed(slot):
+                    c.wait_send()
+
+        @pl.when((local == owner) & (half == 1))
         def _():
-            copy(slot, 1, (prow + 1) % N_PROW).wait_recv()
-    t_ref[:, :B] = t0[...]
-    t_ref[:, B:] = t1[...]
-    c_ref[...] = tc[...]
-
-
-def gather_sites(pk):
+            pl.semaphore_wait(barrier, HALF - 1)
+            copies = spread(slot, owner, True)
+            for c in copies[:len(pieces(slot, zlo))]:
+                c.wait_recv()
+            for c in copies:
+                c.start()
+            for c in copies:
+                c.wait_send()
+
+    for slot, owner in enumerate(owners):
+        @pl.when(local != owner)
+        def _():
+            for c in spread(slot, owner, False)[:len(pieces(slot, zlo))]:
+                c.wait_recv()
+    for slot, (xy, ob) in enumerate(((xy0, ob0), (xy1, ob1))):
+        at = slice(slot * B, slot * B + B)
+        t_ref[0:1, at] = xy[0, 0:1, :]
+        t_ref[1:2, at] = xy[1, 0:1, :]
+        t_ref[2:3, at] = ob[0:1, :]
+    c_ref[0:1, :] = xyc[0, 0:1, :]
+    c_ref[1:2, :] = xyc[1, 0:1, :]
+
+
+def gather_sites(coords, observations):
     vm = pl.BlockSpec(memory_space=pltpu.VMEM)
+    stay = pl.BlockSpec(memory_space=pl.ANY)
     return pl.pallas_call(
         gather_kernel,
         out_shape=(jax.ShapeDtypeStruct((4, T), F32), jax.ShapeDtypeStruct((4, NC), F32)),
-        in_specs=[vm], out_specs=(vm, vm),
+        in_specs=[stay, stay], out_specs=(vm, vm),
         scratch_shapes=[
-            pltpu.VMEM((4, B), F32), pltpu.VMEM((4, B), F32), pltpu.VMEM((4, NC), F32),
-            pltpu.SemaphoreType.DMA((N_PROW,)), pltpu.SemaphoreType.DMA((3,)),
+            pltpu.VMEM((2, 8, B), F32), pltpu.VMEM((2, 8, B), F32), pltpu.VMEM((2, 8, NC), F32),
+            pltpu.VMEM((8, B), F32), pltpu.VMEM((8, B), F32),
+            pltpu.SemaphoreType.DMA((HALF, 2)), pltpu.SemaphoreType.DMA((2, 2)),
+            pltpu.SemaphoreType.DMA((3, 2)), pltpu.SemaphoreType.DMA((2,)),
         ],
         compiler_params=pltpu.CompilerParams(collective_id=0, has_side_effects=True),
         name="gather_sites",
-    )(pk)
+    )(coords, observations)
 
 
 def split(x):
@@ -324,8 +397,7 @@
 
 
 def shards(coords, observations, length_scale, nugget):
-    pk = jnp.concatenate([coords[:, 0, :], observations[0:1], observations[0:1]], 0)
-    sites, columns = gather_sites(pk)
+    sites, columns = gather_sites(coords, observations)
     slab, white, ll = main_call(length_scale, nugget, coords, observations, sites, columns)
     return slab, white, ll[0, :1]
 

time: 67.7 us -> 63.5 us (0.938)
  Pallas kernels: 63.4 us -> 60.6 us
  local copies, waits for them, and re-layouts: 1.49 us -> 0 us
    pallas_call x1, Pallas kernels: 14.7 us -> 11.9 us  [gather_sites(): pl.pallas_call(gather_kernel, out_shape=(jax.ShapeDtypeStruct((4, T), F32...]
    slice x2 -> x0, local copies, waits for them, and re-layouts: 1.48 us -> none  [the longest x1 0.76 us: shards(): coords[:, 0, :]]
where the time goes in v4:
time: 63.5 us; the launch traced here: 62.5 us
  Pallas kernels  60.6 us (95%)
  between operations  1.93 us (3%)
    pallas_call x1, Pallas kernels, main_call(): pl.pallas_call(main_kernel, out_shape=(jax.ShapeDtypeStruct((TILES, B, NC...  48.7 us
    pallas_call x1, Pallas kernels, gather_sites(): pl.pallas_call(gather_kernel, out_shape=(jax.ShapeDtypeStruct((4, T), F32...  11.9 us

profile of v4, /device:TPU:1, one launch (start us, length us, event | category | flops | bytes accessed | tf_op | source)
XLA Modules:
  0.0 62.5 jit_solution(15609503430979767110)
XLA Ops:
  1.9 11.9 %gather_sites.1 = (f32[4,1024]{1,0:T(4,128)}, f32[4,128]{1,0:T(4,128)}) custom-call(f32[2,8,512]{2,1,0:T(8,128)} %co_ref.3, f32[8,512]{1,0:T(8,128)} %ob_ref.3), custom_call_target="tpu_custom_call" | custom-call | tf_op jit(solution)/shard_map/gather_sites/pallas_call | solution.py:140
  13.9 48.7 %factor_and_slab.1 = (f32[8,512,128]{2,1,0:T(8,128)}, f32[8,512]{1,0:T(8,128)}, f32[1,128]{1,0:T(1,128)}) custom-call(f32[1]{0:T(128)S(6)} %copy.7.ls_ref, f32[1]{0:T(128)S(6)} %copy.8.ng_ref, f32[2,8,512]{2,1,0:T(8,128)} %co_ref.3, f32[8,512]{1,0:T(8,128)} %ob_ref.3, f32[4,1024]{1,0:T(4,128)} %get-tuple-element.8.t_ref, f32[4,128]{1,0:T(4,128)} %get-tuple-element.9.c_ref), custom_call_target="tpu_custom_call" | custom-call | tf_op jit(solution)/shard_map/factor_and_slab/pallas_call | solution.py:371

commit v5 on v4

--- a/solution.py
+++ b/solution.py
@@ -237,7 +237,7 @@
 def main_kernel(ls_ref, ng_ref, co_ref, ob_ref, t_ref, c_ref,
                 slab_ref, white_ref, ll_ref,
                 a_ref, w_ref, wt_ref, yh_ref, yl_ref, yb_ref, z_ref, m_ref,
-                rx_ref, ry_ref, mc_ref, wv_ref, ld_ref, flat_ref, d_ref):
+                rx_ref, ry_ref, mc_ref, wv_ref, ld_ref, flat_ref, d_ref, px_ref, py_ref, fx_ref, fy_ref):
     prow = lax.axis_index("prow")
     pcol = lax.axis_index("pcol")
     rate = SQRT_THREE / jnp.full((1, 128), ls_ref[0], F32)
@@ -254,33 +254,39 @@
 
     for q in range(TILES):
         for i in range(4):
+            at = slice(4 * q + i, 4 * q + i + 1)
             part = slice(128 * i, 128 * i + 128)
-            at = slice(q * B + 128 * i, q * B + 128 * i + 128)
-            rx_ref[at, :] = jnp.broadcast_to(co_ref[0, q:q + 1, part] * rate, (128, 128)).T
-            ry_ref[at, :] = jnp.broadcast_to(co_ref[1, q:q + 1, part] * rate, (128, 128)).T
-            flat_ref[4 * q + i:4 * q + i + 1, :] = ob_ref[q:q + 1, part]
-
+            flat_ref[at, :] = ob_ref[q:q + 1, part]
+            fx_ref[at, :] = co_ref[0, q:q + 1, part] * rate
+            fy_ref[at, :] = co_ref[1, q:q + 1, part] * rate
+
+    def spread_tile(slot, q):
+        for i in range(4):
+            part = slice(128 * i, 128 * i + 128)
+            rx_ref[slot, part, :] = jnp.broadcast_to(fx_ref[pl.ds(4 * q + i, 1), :], (128, 128)).T
+            ry_ref[slot, part, :] = jnp.broadcast_to(fy_ref[pl.ds(4 * q + i, 1), :], (128, 128)).T
+
+    wide = lax.broadcasted_iota(jnp.int32, (128, 128), 1)
     for k in range(NK):
         part = slice(128 * k, 128 * k + 128)
-        px = jnp.broadcast_to(tx[:, part], (128, 128)).T
-        py = jnp.broadcast_to(ty[:, part], (128, 128)).T
-        w_ref[0] = px
-        w_ref[1] = py
-        wide = lax.broadcasted_iota(jnp.int32, (128, 128), 1)
+        px_ref[part, :] = jnp.broadcast_to(tx[:, part], (128, 128)).T
+        py_ref[part, :] = jnp.broadcast_to(ty[:, part], (128, 128)).T
         a_ref[k, :, T + NC:] = jnp.where(
             wide == 0, jnp.broadcast_to(t_ref[2:3, part], (128, 128)).T, 0.0)
-
+    spread_tile(0, 0)
+    for k in range(NK):
         def build(g, carry, k=k):
-            at = pl.ds(pl.multiple_of(8 * g, 8), 8)
-            gx = w_ref[0, at, :]
-            gy = w_ref[1, at, :]
-            for j in range(k, 9):
-                v = matern(gx - ux[j], gy - uy[j])
-                if j == k:
-                    v = v + jnp.where(lane == sub + 8 * g, nugget, 0.0)
-                a_ref[k, at, 128 * j:128 * j + 128] = v
+            for e in range(4):
+                r = pl.multiple_of(32 * g + 8 * e, 8)
+                gx = px_ref[pl.ds(128 * k + r, 8), :]
+                gy = py_ref[pl.ds(128 * k + r, 8), :]
+                for j in range(k, 9):
+                    v = matern(gx - ux[j], gy - uy[j])
+                    if j == k:
+                        v = v + jnp.where(lane == sub + r, nugget, 0.0)
+                    a_ref[k, pl.ds(r, 8), 128 * j:128 * j + 128] = v
             return carry
-        lax.fori_loop(0, 16, build, 0)
+        lax.fori_loop(0, 4, build, 0)
 
     ld_ref[...] = jnp.zeros((8, 128), F32)
 
@@ -322,8 +328,10 @@
         m_ref[128 * k:128 * k + 128, :] = mm3(wt_ref[k], acc)
 
     mh, ml = split(m_ref[:, :NC])
-    mc_ref[:, :NC] = mh
-    mc_ref[:, NC:] = ml
+    mc_ref[:T, :NC] = mh
+    mc_ref[:T, NC:] = ml
+    mc_ref[T:, :NC] = mh
+    mc_ref[T:, NC:] = jnp.zeros((T, NC), BF16)
     wt = m_ref[:, NC:].T
     wh, wl = split(wt[0:1, :])
     wv_ref[...] = jnp.concatenate([wh, wl, jnp.zeros((14, T), BF16)], 0)
@@ -332,33 +340,34 @@
     total = jnp.sum(z * z) + jnp.sum(ld_ref[:, 0:1])
     ll_ref[...] = jnp.full((1, 128), total * (-0.5 / T), F32)
 
-    wl_ = lax.broadcasted_iota(jnp.int32, (128, 128), 1)
     ws_ = lax.broadcasted_iota(jnp.int32, (128, 128), 0)
 
     def body(q, carry):
         panel = (q == 0) & (prow < 2)
+        slot = q % 2
+        spread_tile(1 - slot, jnp.minimum(q + 1, TILES - 1))
         for j in range(4):
-            at = pl.ds(pl.multiple_of(512 * q + 128 * j, 128), 128)
-            gx = rx_ref[at, :]
-            gy = ry_ref[at, :]
-            acc = None
-            for t in range(4):
-                piece = jnp.concatenate(
-                    [matern(gx - ux[2 * t + e], gy - uy[2 * t + e]) for e in range(2)], 1)
-                ch, cl = split(piece)
-                mt = mc_ref[256 * t:256 * t + 256, :]
-                wv = wv_ref[:, 256 * t:256 * t + 256]
-                both = mm(ch, mt)
-                low = mm(cl, mt[:, :NC])
-                wr = lax.dot_general(wv, ch, (((1,), (1,)), ((), ())), preferred_element_type=F32)
-                wr2 = lax.dot_general(wv, cl, (((1,), (1,)), ((), ())), preferred_element_type=F32)
-                cur = (both[:, :NC] + both[:, NC:] + low, wr[0:1] + wr[1:2] + wr2[0:1])
-                acc = cur if acc is None else (acc[0] + cur[0], acc[1] + cur[1])
+            rows_j = slice(128 * j, 128 * j + 128)
+            gx = rx_ref[slot, rows_j, :]
+            gy = ry_ref[slot, rows_j, :]
+            high, low = [], []
+            for t in range(8):
+                ch, cl = split(matern(gx - ux[t], gy - uy[t]))
+                high.append(ch)
+                low.append(cl)
+            ch = jnp.concatenate(high, 1)
+            cl = jnp.concatenate(low, 1)
+            both = mm(jnp.concatenate([ch, cl], 1), mc_ref[...])
+            nt = (((1,), (1,)), ((), ()))
+            wr = lax.dot_general(wv_ref[...], ch, nt, preferred_element_type=F32)
+            wr2 = lax.dot_general(wv_ref[...], cl, nt, preferred_element_type=F32)
             first = (q * N_PROW + prow) * B + 128 * j - (T + pcol * NC)
-            value = matern(gx - cx, gy - cy) + jnp.where(wl_ == ws_ + first, nugget, 0.0) - acc[0]
-            slab_ref[q, 128 * j:128 * j + 128, :] = jnp.where(panel, 0.0, value)
+            value = matern(gx - cx, gy - cy) + jnp.where(wide == ws_ + first, nugget, 0.0)
+            value = value - both[:, :NC] - both[:, NC:]
+            slab_ref[q, rows_j, :] = jnp.where(panel, 0.0, value)
             zr = z_ref[pl.ds(jnp.minimum(prow, 1) * 4 + j, 1), :]
-            flat_ref[pl.ds(4 * q + j, 1), :] = jnp.where(panel, zr, flat_ref[pl.ds(4 * q + j, 1), :] - acc[1])
+            at = pl.ds(4 * q + j, 1)
+            flat_ref[at, :] = jnp.where(panel, zr, flat_ref[at, :] - (wr[0:1] + wr[1:2] + wr2[0:1]))
         return carry
     lax.fori_loop(0, TILES, body, 0)
     for r in range(32):
@@ -383,13 +392,17 @@
             pltpu.VMEM((NK, NB, 2 * NC), F32),
             pltpu.VMEM((NK, NB), F32),
             pltpu.VMEM((T, 2 * NC), F32),
-            pltpu.VMEM((TILES * B, 128), F32),
-            pltpu.VMEM((TILES * B, 128), F32),
-            pltpu.VMEM((T, 2 * NC), BF16),
+            pltpu.VMEM((2, B, 128), F32),
+            pltpu.VMEM((2, B, 128), F32),
+            pltpu.VMEM((2 * T, 2 * NC), BF16),
             pltpu.VMEM((16, T), BF16),
             pltpu.VMEM((8, 128), F32),
             pltpu.VMEM((32, 128), F32),
             pltpu.VMEM((NB, NB), F32),
+            pltpu.VMEM((T, 128), F32),
+            pltpu.VMEM((T, 128), F32),
+            pltpu.VMEM((32, 128), F32),
+            pltpu.VMEM((32, 128), F32),
         ],
         compiler_params=pltpu.CompilerParams(vmem_limit_bytes=60 * 1024 * 1024),
         name="factor_and_slab",

time: 63.5 us -> 61.3 us (0.965)
  Pallas kernels: 60.6 us -> 58.5 us
    pallas_call x1, Pallas kernels: 48.7 us -> 46.5 us  [main_call(): pl.pallas_call(main_kernel, out_shape=(jax.ShapeDtypeStruct((TILES, B, NC...]
where the time goes in v5:
time: 61.3 us; the launch traced here: 60.4 us
  Pallas kernels  58.5 us (95%)
  between operations  1.93 us (3%)
    pallas_call x1, Pallas kernels, main_call(): pl.pallas_call(main_kernel, out_shape=(jax.ShapeDtypeStruct((TILES, B, NC...  46.5 us
    pallas_call x1, Pallas kernels, gather_sites(): pl.pallas_call(gather_kernel, out_shape=(jax.ShapeDtypeStruct((4, T), F32...  11.9 us

profile of v5, /device:TPU:1, one launch (start us, length us, event | category | flops | bytes accessed | tf_op | source)
XLA Modules:
  0.0 60.4 jit_solution(8281996872680400820)
XLA Ops:
  1.9 11.9 %gather_sites.1 = (f32[4,1024]{1,0:T(4,128)}, f32[4,128]{1,0:T(4,128)}) custom-call(f32[2,8,512]{2,1,0:T(8,128)} %co_ref.3, f32[8,512]{1,0:T(8,128)} %ob_ref.3), custom_call_target="tpu_custom_call" | custom-call | tf_op jit(solution)/shard_map/gather_sites/pallas_call | solution.py:140
  13.9 46.5 %factor_and_slab.1 = (f32[8,512,128]{2,1,0:T(8,128)}, f32[8,512]{1,0:T(8,128)}, f32[1,128]{1,0:T(1,128)}) custom-call(f32[1]{0:T(128)S(6)} %copy.7.ls_ref, f32[1]{0:T(128)S(6)} %copy.8.ng_ref, f32[2,8,512]{2,1,0:T(8,128)} %co_ref.3, f32[8,512]{1,0:T(8,128)} %ob_ref.3, f32[4,1024]{1,0:T(4,128)} %get-tuple-element.8.t_ref, f32[4,128]{1,0:T(4,128)} %get-tuple-element.9.c_ref), custom_call_target="tpu_custom_call" | custom-call | tf_op jit(solution)/shard_map/factor_and_slab/pallas_call | solution.py:380

commit v6 on v5

--- a/solution.py
+++ b/solution.py
@@ -16,7 +16,7 @@
 B = 512
 T = 2 * B
 NB = 128
-SP = 64
+SP = 32
 PW = 16
 NK = T // NB
 N_PROW = 16
@@ -198,23 +198,28 @@
             for v in range(c0 // 8, nv):
                 fill = jnp.where((lane - r0) == (sub + 8 * v), 1.0, 0.0) if v in own else 0.0
                 a[v] = jnp.where(group, fill, a[v])
-            for t in range(c0, c0 + PW):
+            for t in range(c0, c0 + PW, 2):
                 vt, st = t // 8, t % 8
-                pivot = rows(cols[t, vt], st)
-                d[vt] = jnp.where(sub == st, pivot, d[vt])
-                rp = 1.0 / pivot
-                m = {v: cols[t, v] * rp for v in range(vt, nv)}
-                for i in range(t + 1, c0 + PW):
-                    entry = rows(cols[t, i // 8], i % 8)
+                p0 = rows(cols[t, vt], st)
+                side = rows(cols[t, vt], st + 1)
+                det = p0 * rows(cols[t + 1, vt], st + 1) - side * side
+                inv0 = 1.0 / p0
+                inv1 = p0 * (1.0 / det)
+                d[vt] = jnp.where(sub == st, p0, jnp.where(sub == st + 1, det * inv0, d[vt]))
+                m0 = {v: cols[t, v] * inv0 for v in range(vt, nv)}
+                for v in range(vt, nv):
+                    cols[t + 1, v] = cols[t + 1, v] - m0[v] * side
+                m1 = {v: cols[t + 1, v] * inv1 for v in range(vt, nv)}
+                for i in range(t + 2, c0 + PW):
+                    e0 = rows(cols[t, i // 8], i % 8)
+                    e1 = rows(cols[t + 1, i // 8], i % 8)
                     for v in range(i // 8, nv):
-                        if i == t + 1 and v == i // 8:
-                            cols[i, v] = cols[i, v] - (cols[t, v] * entry) * rp
-                        else:
-                            cols[i, v] = cols[i, v] - m[v] * entry
-                row = rows(a[vt], st)
-                for v in range(vt, nv):
-                    mv = jnp.where(sub > st, m[v], 0.0) if v == vt else m[v]
-                    a[v] = a[v] - mv * row
+                        cols[i, v] = (cols[i, v] - m0[v] * e0) - m1[v] * e1
+                for step, m in ((st, m0), (st + 1, m1)):
+                    row = rows(a[vt], step)
+                    for v in range(vt, nv):
+                        mv = jnp.where(sub > step, m[v], 0.0) if v == vt else m[v]
+                        a[v] = a[v] - mv * row
         y_out = []
         for v in range(nv):
             y = a[v] * lax.rsqrt(d[v])
@@ -224,9 +229,9 @@
         w_ref[k, r0:r0 + SP, :] = jnp.where(wide < r0 + SP, y, 0.0)
         if r0 + SP < NB:
             yh, yl = split(y)
-            left = jnp.concatenate([yh.astype(F32), yh.astype(F32), yl.astype(F32)], 0).T
-            left = left[r0 + SP:, :].astype(BF16)
-            update = mm(left, jnp.concatenate([yh, yl, yh], 0))
+            update = lax.dot_general(
+                jnp.concatenate([yh, yh, yl], 0), jnp.concatenate([yh, yl, yh], 0),
+                (((0,), (0,)), ((), ())), preferred_element_type=F32)[r0 + SP:, :]
             rest = d_ref[r0 + SP:, :]
             own = lax.broadcasted_iota(jnp.int32, rest.shape, 1)
             own = (own >= r0) & (own < r0 + SP)

time: 61.3 us -> 60.2 us (0.982)
  Pallas kernels: 58.5 us -> 57.4 us
    pallas_call x1, Pallas kernels: 46.5 us -> 45.4 us  [main_call(): pl.pallas_call(main_kernel, out_shape=(jax.ShapeDtypeStruct((TILES, B, NC...]
where the time goes in v6:
time: 60.2 us; the launch traced here: 59.3 us
  Pallas kernels  57.4 us (95%)
  between operations  1.93 us (3%)
    pallas_call x1, Pallas kernels, main_call(): pl.pallas_call(main_kernel, out_shape=(jax.ShapeDtypeStruct((TILES, B, NC...  45.4 us
    pallas_call x1, Pallas kernels, gather_sites(): pl.pallas_call(gather_kernel, out_shape=(jax.ShapeDtypeStruct((4, T), F32...  11.9 us

profile of v6, /device:TPU:1, one launch (start us, length us, event | category | flops | bytes accessed | tf_op | source)
XLA Modules:
  0.0 59.3 jit_solution(7784816648006942734)
XLA Ops:
  1.9 11.9 %gather_sites.1 = (f32[4,1024]{1,0:T(4,128)}, f32[4,128]{1,0:T(4,128)}) custom-call(f32[2,8,512]{2,1,0:T(8,128)} %co_ref.3, f32[8,512]{1,0:T(8,128)} %ob_ref.3), custom_call_target="tpu_custom_call" | custom-call | tf_op jit(solution)/shard_map/gather_sites/pallas_call | solution.py:140
  13.9 45.4 %factor_and_slab.1 = (f32[8,512,128]{2,1,0:T(8,128)}, f32[8,512]{1,0:T(8,128)}, f32[1,128]{1,0:T(1,128)}) custom-call(f32[1]{0:T(128)S(6)} %copy.7.ls_ref, f32[1]{0:T(128)S(6)} %copy.8.ng_ref, f32[2,8,512]{2,1,0:T(8,128)} %co_ref.3, f32[8,512]{1,0:T(8,128)} %ob_ref.3, f32[4,1024]{1,0:T(4,128)} %get-tuple-element.8.t_ref, f32[4,128]{1,0:T(4,128)} %get-tuple-element.9.c_ref), custom_call_target="tpu_custom_call" | custom-call | tf_op jit(solution)/shard_map/factor_and_slab/pallas_call | solution.py:385

commit v7 on v6

--- a/solution.py
+++ b/solution.py
@@ -279,6 +279,7 @@
         a_ref[k, :, T + NC:] = jnp.where(
             wide == 0, jnp.broadcast_to(t_ref[2:3, part], (128, 128)).T, 0.0)
     spread_tile(0, 0)
+    spread_tile(1, 1)
     for k in range(NK):
         def build(g, carry, k=k):
             for e in range(4):
@@ -315,11 +316,12 @@
                 yb_ref[kk] = y[:, n - 256:]
                 z_ref[kk:kk + 1, :] = y[:, n - 128:].T[0:1, :]
                 ycat = jnp.concatenate([yh, yl, yh], 0)
+                tcat = jnp.concatenate([yh, yh, yl], 0)
                 for i in range(kk + 1, NK):
                     f = 128 * (i - kk - 1)
-                    th, tl = split(y[:, f:f + 128].T)
-                    tcat = jnp.concatenate([th, th, tl], 1)
-                    a_ref[i, :, 128 * i:] = a_ref[i, :, 128 * i:] - mm(tcat, ycat[:, f:])
+                    a_ref[i, :, 128 * i:] = a_ref[i, :, 128 * i:] - lax.dot_general(
+                        tcat[:, f:f + 128], ycat[:, f:], (((0,), (0,)), ((), ())),
+                        preferred_element_type=F32)
         return carry
     lax.fori_loop(0, NK, step, 0)
 
@@ -347,34 +349,36 @@
 
     ws_ = lax.broadcasted_iota(jnp.int32, (128, 128), 0)
 
-    def body(q, carry):
-        panel = (q == 0) & (prow < 2)
-        slot = q % 2
-        spread_tile(1 - slot, jnp.minimum(q + 1, TILES - 1))
-        for j in range(4):
-            rows_j = slice(128 * j, 128 * j + 128)
-            gx = rx_ref[slot, rows_j, :]
-            gy = ry_ref[slot, rows_j, :]
-            high, low = [], []
-            for t in range(8):
-                ch, cl = split(matern(gx - ux[t], gy - uy[t]))
-                high.append(ch)
-                low.append(cl)
-            ch = jnp.concatenate(high, 1)
-            cl = jnp.concatenate(low, 1)
-            both = mm(jnp.concatenate([ch, cl], 1), mc_ref[...])
-            nt = (((1,), (1,)), ((), ()))
-            wr = lax.dot_general(wv_ref[...], ch, nt, preferred_element_type=F32)
-            wr2 = lax.dot_general(wv_ref[...], cl, nt, preferred_element_type=F32)
-            first = (q * N_PROW + prow) * B + 128 * j - (T + pcol * NC)
-            value = matern(gx - cx, gy - cy) + jnp.where(wide == ws_ + first, nugget, 0.0)
-            value = value - both[:, :NC] - both[:, NC:]
-            slab_ref[q, rows_j, :] = jnp.where(panel, 0.0, value)
-            zr = z_ref[pl.ds(jnp.minimum(prow, 1) * 4 + j, 1), :]
-            at = pl.ds(4 * q + j, 1)
-            flat_ref[at, :] = jnp.where(panel, zr, flat_ref[at, :] - (wr[0:1] + wr[1:2] + wr2[0:1]))
+    def body(pair, carry):
+        for e in range(2):
+            q = 2 * pair + e
+            panel = (q == 0) & (prow < 2)
+            slot = 2 * (pair % 2) + e
+            spread_tile(2 * (1 - pair % 2) + e, jnp.minimum(q + 2, TILES - 1))
+            for j in range(4):
+                rows_j = slice(128 * j, 128 * j + 128)
+                gx = rx_ref[slot, rows_j, :]
+                gy = ry_ref[slot, rows_j, :]
+                high, low = [], []
+                for t in range(8):
+                    ch, cl = split(matern(gx - ux[t], gy - uy[t]))
+                    high.append(ch)
+                    low.append(cl)
+                ch = jnp.concatenate(high, 1)
+                cl = jnp.concatenate(low, 1)
+                both = mm(jnp.concatenate([ch, cl], 1), mc_ref[...])
+                nt = (((1,), (1,)), ((), ()))
+                wr = lax.dot_general(wv_ref[...], ch, nt, preferred_element_type=F32)
+                wr2 = lax.dot_general(wv_ref[...], cl, nt, preferred_element_type=F32)
+                first = (q * N_PROW + prow) * B + 128 * j - (T + pcol * NC)
+                value = matern(gx - cx, gy - cy) + jnp.where(wide == ws_ + first, nugget, 0.0)
+                value = value - both[:, :NC] - both[:, NC:]
+                slab_ref[q, rows_j, :] = jnp.where(panel, 0.0, value)
+                zr = z_ref[pl.ds(jnp.minimum(prow, 1) * 4 + j, 1), :]
+                at = pl.ds(4 * q + j, 1)
+                flat_ref[at, :] = jnp.where(panel, zr, flat_ref[at, :] - (wr[0:1] + wr[1:2] + wr2[0:1]))
         return carry
-    lax.fori_loop(0, TILES, body, 0)
+    lax.fori_loop(0, TILES // 2, body, 0)
     for r in range(32):
         white_ref[r // 4:r // 4 + 1, 128 * (r % 4):128 * (r % 4) + 128] = flat_ref[r:r + 1, :]
 
@@ -397,8 +401,8 @@
             pltpu.VMEM((NK, NB, 2 * NC), F32),
             pltpu.VMEM((NK, NB), F32),
             pltpu.VMEM((T, 2 * NC), F32),
-            pltpu.VMEM((2, B, 128), F32),
-            pltpu.VMEM((2, B, 128), F32),
+            pltpu.VMEM((4, B, 128), F32),
+            pltpu.VMEM((4, B, 128), F32),
             pltpu.VMEM((2 * T, 2 * NC), BF16),
             pltpu.VMEM((16, T), BF16),
             pltpu.VMEM((8, 128), F32),

time: 60.2 us -> 59.4 us (0.987)
  Pallas kernels: 57.4 us -> 56.6 us
    pallas_call x1, Pallas kernels: 45.4 us -> 44.6 us  [main_call(): pl.pallas_call(main_kernel, out_shape=(jax.ShapeDtypeStruct((TILES, B, NC...]
where the time goes in v7:
time: 59.4 us; the launch traced here: 58.5 us
  Pallas kernels  56.6 us (95%)
  between operations  1.93 us (3%)
    pallas_call x1, Pallas kernels, main_call(): pl.pallas_call(main_kernel, out_shape=(jax.ShapeDtypeStruct((TILES, B, NC...  44.6 us
    pallas_call x1, Pallas kernels, gather_sites(): pl.pallas_call(gather_kernel, out_shape=(jax.ShapeDtypeStruct((4, T), F32...  11.9 us

profile of v7, /device:TPU:1, one launch (start us, length us, event | category | flops | bytes accessed | tf_op | source)
XLA Modules:
  0.0 58.5 jit_solution(9743916135731938035)
XLA Ops:
  1.9 11.9 %gather_sites.1 = (f32[4,1024]{1,0:T(4,128)}, f32[4,128]{1,0:T(4,128)}) custom-call(f32[2,8,512]{2,1,0:T(8,128)} %co_ref.3, f32[8,512]{1,0:T(8,128)} %ob_ref.3), custom_call_target="tpu_custom_call" | custom-call | tf_op jit(solution)/shard_map/gather_sites/pallas_call | solution.py:140
  13.9 44.6 %factor_and_slab.1 = (f32[8,512,128]{2,1,0:T(8,128)}, f32[8,512]{1,0:T(8,128)}, f32[1,128]{1,0:T(1,128)}) custom-call(f32[1]{0:T(128)S(6)} %copy.7.ls_ref, f32[1]{0:T(128)S(6)} %copy.8.ng_ref, f32[2,8,512]{2,1,0:T(8,128)} %co_ref.3, f32[8,512]{1,0:T(8,128)} %ob_ref.3, f32[4,1024]{1,0:T(4,128)} %get-tuple-element.8.t_ref, f32[4,128]{1,0:T(4,128)} %get-tuple-element.9.c_ref), custom_call_target="tpu_custom_call" | custom-call | tf_op jit(solution)/shard_map/factor_and_slab/pallas_call | solution.py:389
